TPU v7x, 512 devices: a whole 4x8x8 slice. The times are simulated.
512 devices in a mesh: grp: 8 (over z_lo, core), cell: 64 (over x, z_hi, y).
Axes of the slice: x: 4, y: 8, z: 8 (z_hi: 2, z_lo: 4; z = z_hi * 4 + z_lo), core: 2. Of those that a mesh axis runs over, the one named last changes fastest.
Arguments:
- row_embed: bfloat16 [8, 128, 64, 512], P('grp', 'cell'), may hold values from -16 to 16
- cotangent: bfloat16 [8, 128, 64, 512], P('grp', 'cell'), may hold values from -16 to 16
- w_qkv: bfloat16 [1536, 512], replicated, may hold values from -0.25 to 0.25
- w_out: bfloat16 [512, 512], replicated, may hold values from -0.25 to 0.25
- treat_vec: float32 [512], replicated, may hold values from -3 to 3
- is_train: int32 [8, 128], P('grp'), may hold values 0 or 1
- treated: int32 [8, 128], P('grp'), may hold values 0 or 1
- block_pattern: int32 [4, 4], replicated, may hold values 0 or 1
Outputs:
- out: bfloat16 [8, 128, 64, 512], P('grp', 'cell')
- grad_input: bfloat16 [8, 128, 64, 512], P('grp', 'cell')
- weight_grads: float32 [2048, 512], P('cell')
All inputs are finite; a program needn't handle non-finite values. No bound on the sum of `is_train` or of `treated` on one device may be relied on, other than what follows from the above.
Results may differ from a plain program's by a relative error of at most 0.014.
The roundings to bfloat16 on the way count: a program that leaves them out, or rounds other values in their place, can miss the bound.
Values may be sent and summed in bfloat16 or wider, within the bound.
No kernel may reach another device: no remote copies, remote signals or barrier semaphores. Data moves between devices by JAX's collectives and lax.ppermute only.
A program may use at most 64 MiB of HBM per device.

v0:
```python
import math

import jax
import jax.numpy as jnp
from jax import lax
from jax.sharding import PartitionSpec as P

HEADS = 8
BLK = 32


def allowed_keys(train_row, pattern, row_count):
    expanded = jnp.repeat(jnp.repeat(pattern, BLK, axis=0), BLK, axis=1)
    index_row = jnp.arange(row_count)
    diagonal = index_row[:, None] == index_row[None, :]
    return (expanded == 1) & (train_row[None, :] == 1) | diagonal


def to_pairs(heads, row_count, feat_local, head_dim):
    return jnp.transpose(heads, (1, 2, 0, 3)).reshape(feat_local * HEADS, row_count, head_dim)


def from_pairs(pairs, row_count, feat_local, head_dim):
    return jnp.transpose(
        pairs.reshape(feat_local, HEADS, row_count, head_dim), (2, 0, 1, 3)
    ).reshape(row_count, feat_local, HEADS * head_dim)


def per_device(row_embed, cotangent, w_qkv, w_out, treat_vec, is_train, treated, block_pattern):
    cell_count = lax.axis_size("cell")
    group_count = lax.axis_size("grp")
    row_dev = row_embed.shape[1]
    feat_count = row_embed.shape[2]
    model_width = row_embed.shape[3]
    row_count = row_dev * cell_count
    head_dim = model_width // HEADS
    scale = 1.0 / math.sqrt(head_dim)
    row_start = lax.axis_index("cell") * row_dev
    my_treat = lax.dynamic_slice_in_dim(treated, row_start, row_dev, 1).astype(jnp.float32)
    shifted = (row_embed.astype(jnp.float32) + my_treat[:, :, None, None] * treat_vec).astype(
        jnp.bfloat16
    )
    shift_cols, grad_cols = (
        lax.all_to_all(shifted, "cell", split_axis=2, concat_axis=1, tiled=True),
        lax.all_to_all(cotangent, "cell", split_axis=2, concat_axis=1, tiled=True),
    )
    shift_local = shift_cols[0]
    grad_local = grad_cols[0]
    feat_local = shift_local.shape[1]
    projected = jnp.einsum(
        "rfd,ed->rfe", shift_local, w_qkv, preferred_element_type=jnp.float32
    ).astype(jnp.bfloat16)
    query_heads = projected[..., :model_width].reshape(row_count, feat_local, HEADS, head_dim)
    key_heads = projected[..., model_width : 2 * model_width].reshape(
        row_count, feat_local, HEADS, head_dim
    )
    value_heads = projected[..., 2 * model_width :].reshape(row_count, feat_local, HEADS, head_dim)
    grad_attended = jnp.einsum(
        "rfe,ed->rfd", grad_local, w_out, preferred_element_type=jnp.float32
    ).astype(jnp.bfloat16)
    grad_att_heads = grad_attended.reshape(row_count, feat_local, HEADS, head_dim)
    allowed = allowed_keys(is_train[0], block_pattern, row_count)

    def attend_pair(items):
        query, keys, values, grad_att = items
        scores = (
            lax.dot_general(
                query, keys, (((1,), (1,)), ((), ())), preferred_element_type=jnp.float32
            )
            * scale
        )
        scores = jnp.where(allowed, scores, -jnp.inf)
        row_peak = jnp.max(scores, axis=-1, keepdims=True)
        exp_scores = jnp.exp(scores - row_peak)
        attn_prob = exp_scores / jnp.sum(exp_scores, axis=-1, keepdims=True)
        prob_b = attn_prob.astype(jnp.bfloat16)
        attended_pair = jnp.dot(prob_b, values, preferred_element_type=jnp.float32).astype(
            jnp.bfloat16
        )
        grad_prob = lax.dot_general(
            grad_att, values, (((1,), (1,)), ((), ())), preferred_element_type=jnp.float32
        )
        row_delta = jnp.sum(attn_prob * grad_prob, axis=-1, keepdims=True)
        grad_score = (attn_prob * (grad_prob - row_delta) * scale).astype(jnp.bfloat16)
        grad_query = jnp.dot(grad_score, keys, preferred_element_type=jnp.float32).astype(
            jnp.bfloat16
        )
        grad_key = lax.dot_general(
            grad_score, query, (((0,), (0,)), ((), ())), preferred_element_type=jnp.float32
        ).astype(jnp.bfloat16)
        grad_value = lax.dot_general(
            prob_b, grad_att, (((0,), (0,)), ((), ())), preferred_element_type=jnp.float32
        ).astype(jnp.bfloat16)
        return (attended_pair, grad_query, grad_key, grad_value)

    pair_inputs = (
        to_pairs(query_heads, row_count, feat_local, head_dim),
        to_pairs(key_heads, row_count, feat_local, head_dim),
        to_pairs(value_heads, row_count, feat_local, head_dim),
        to_pairs(grad_att_heads, row_count, feat_local, head_dim),
    )
    att_pairs, gq_pairs, gk_pairs, gv_pairs = lax.map(attend_pair, pair_inputs)
    attended = from_pairs(att_pairs, row_count, feat_local, head_dim)
    output = (
        shift_local.astype(jnp.float32)
        + jnp.einsum("rfd,ed->rfe", attended, w_out, preferred_element_type=jnp.float32)
    ).astype(jnp.bfloat16)
    grad_projected = jnp.concatenate(
        [
            from_pairs(gq_pairs, row_count, feat_local, head_dim),
            from_pairs(gk_pairs, row_count, feat_local, head_dim),
            from_pairs(gv_pairs, row_count, feat_local, head_dim),
        ],
        axis=-1,
    )
    grad_in = (
        grad_local.astype(jnp.float32)
        + jnp.einsum("rfe,ed->rfd", grad_projected, w_qkv, preferred_element_type=jnp.float32)
    ).astype(jnp.bfloat16)
    out_rows, grad_rows = (
        lax.all_to_all(output[None], "cell", split_axis=1, concat_axis=2, tiled=True),
        lax.all_to_all(grad_in[None], "cell", split_axis=1, concat_axis=2, tiled=True),
    )
    grad_term = jnp.concatenate(
        [
            jnp.einsum(
                "rfe,rfd->ed", grad_projected, shift_local, preferred_element_type=jnp.float32
            ),
            jnp.einsum("rfe,rfd->ed", grad_local, attended, preferred_element_type=jnp.float32),
        ],
        axis=0,
    )
    share_rows = 4 * model_width // cell_count
    summed_all = lax.psum(grad_term, ("grp", "cell"))
    summed = lax.dynamic_slice_in_dim(
        summed_all, lax.axis_index("cell") * share_rows, share_rows, 0
    )
    gscale = 1.0 / math.sqrt(group_count * row_count * feat_count)
    return (out_rows, grad_rows, summed * gscale)


def solution(mesh):
    return jax.shard_map(
        per_device,
        mesh=mesh,
        in_specs=(
            P("grp", "cell", None, None),
            P("grp", "cell", None, None),
            P(),
            P(),
            P(),
            P("grp", None),
            P("grp", None),
            P(),
        ),
        out_specs=(P("grp", "cell", None, None), P("grp", "cell", None, None), P("cell", None)),
        check_vma=False,
    )
```

profile of v0, /device:TPU:1, one launch (start us, length us, event | category | flops | bytes accessed | tf_op | source)
XLA Modules:
  0.0 370.4 jit_solution(7435198926314266273)
XLA Ops:
  7.2 0.8 convert_bitcast_fusion
  8.0 0.8 broadcast_multiply_fusion
  8.8 0.9 add_convert_fusion
  9.7 0.8 copy.63
  10.5 19.6 %all-to-all-start = ((bf16[1,2,64,512]{3,1,0,2:T(2,128)(2,1)}), bf16[1,2,64,512]{3,1,0,2:T(2,128)(2,1)S(1)}, u32[]{:S(2)}, u32[]{:S(2)}) async-start(bf16[1,2,64,512]{3,1,0,2:T(2,128)(2,1)} %copy.63), calls=%async_computation | async-start | bytes 262144 | tf_op jit(solution)/shard_map/all_to_all | solution.py:44
  30.1 1.7 copy.67
  31.8 12.2 %all-to-all-done = bf16[1,2,64,512]{3,1,0,2:T(2,128)(2,1)S(1)} async-done(((bf16[1,2,64,512]{3,1,0,2:T(2,128)(2,1)}), bf16[1,2,64,512]{3,1,0,2:T(2,128)(2,1)S(1)}, u32[]{:S(2)}, u32[]{:S(2)}) %all-to-all-start) | async-done | bytes 131104 | tf_op jit(solution)/shard_map/all_to_all | solution.py:44
  44.0 4.6 %all-to-all-start.1 = ((bf16[1,2,64,512]{3,1,0,2:T(2,128)(2,1)}), bf16[1,2,64,512]{3,1,0,2:T(2,128)(2,1)S(1)}, u32[]{:S(2)}, u32[]{:S(2)}) async-start(bf16[1,2,64,512]{3,1,0,2:T(2,128)(2,1)} %copy.67), calls=%async_computation.1 | async-start | bytes 262144 | tf_op jit(solution)/shard_map/all_to_all | solution.py:45
  48.7 0.7 broadcast_compare_fusion
  49.6 0.7 compare_bitcast_fusion
  50.4 12.2 %all-to-all-done.1 = bf16[1,2,64,512]{3,1,0,2:T(2,128)(2,1)S(1)} async-done(((bf16[1,2,64,512]{3,1,0,2:T(2,128)(2,1)}), bf16[1,2,64,512]{3,1,0,2:T(2,128)(2,1)S(1)}, u32[]{:S(2)}, u32[]{:S(2)}) %all-to-all-start.1) | async-done | bytes 131104 | tf_op jit(solution)/shard_map/all_to_all | solution.py:45
  62.6 1.3 convolution_convert_fusion.5
  64.0 0.6 fusion.41
  65.1 10.1 %while.17 = (s32[]{:T(128)}, bf16[8,128,64]{1,2,0:T(8,128)(2,1)S(1)}, bf16[8,128,64]{1,2,0:T(8,128)(2,1)S(1)}, bf16[8,128,64]{1,2,0:T(8,128)(2,1)S(1)}, bf16[8,1...) while((s32[]{:T(128)}, ...), condition=%wide.region_4.5_spmd.clone, body=%wide.region_0.4_spmd.clone.sunk | while | flops 13008514 | bytes 865533 | solution.py:102
  65.2 0.2 fusion.85
  65.5 0.2 multiply_reduce_fusion.2
  66.4 0.2 fusion.85
  66.7 0.2 multiply_reduce_fusion.2
  67.7 0.2 fusion.85
  68.0 0.2 multiply_reduce_fusion.2
  69.3 0.2 multiply_reduce_fusion.2
  70.2 0.2 fusion.85
  70.5 0.2 multiply_reduce_fusion.2
  71.5 0.2 fusion.85
  71.8 0.2 multiply_reduce_fusion.2
  73.1 0.2 multiply_reduce_fusion.2
  74.3 0.2 multiply_reduce_fusion.2
  75.2 0.4 convolution_bitcast_fusion
  75.6 0.6 fusion.46
  76.1 2.4 pad_maximum_fusion
  78.6 1.0 copy-done.1
  79.6 0.3 fusion.44
  80.1 0.5 broadcast.46
  80.6 1.4 reduce.4
  82.0 0.7 reshape.155
  82.7 4.6 %all-to-all-start.2 = ((bf16[64,2,512]{2,1,0:T(2,128)(2,1)}), bf16[64,2,512]{2,1,0:T(2,128)(2,1)S(1)}, u32[]{:S(2)}, u32[]{:S(2)}) async-start(bf16[64,2,512]{2,1,0:T(2,128)(2,1)} %reshape.155), calls=%async_computation.2 | async-start | bytes 262144 | tf_op jit(solution)/shard_map/all_to_all | solution.py:121
  87.4 0.4 fusion.45
  88.0 1.4 reduce.5
  89.4 0.7 reshape.157
  90.1 11.6 %all-to-all-done.2 = bf16[64,2,512]{2,1,0:T(2,128)(2,1)S(1)} async-done(((bf16[64,2,512]{2,1,0:T(2,128)(2,1)}), bf16[64,2,512]{2,1,0:T(2,128)(2,1)S(1)}, u32[]{:S(2)}, u32[]{:S(2)}) %all-to-all-start.2) | async-done | bytes 131104 | tf_op jit(solution)/shard_map/all_to_all | solution.py:121
  101.7 4.6 %all-to-all-start.3 = ((bf16[64,2,512]{2,1,0:T(2,128)(2,1)}), bf16[64,2,512]{2,1,0:T(2,128)(2,1)S(1)}, u32[]{:S(2)}, u32[]{:S(2)}) async-start(bf16[64,2,512]{2,1,0:T(2,128)(2,1)} %reshape.157), calls=%async_computation.3 | async-start | bytes 262144 | tf_op jit(solution)/shard_map/all_to_all | solution.py:122
  106.4 0.7 bitcast_reduce_fusion.1
  107.2 0.7 copy.76
  107.9 12.4 %all-to-all-done.3 = bf16[64,2,512]{2,1,0:T(2,128)(2,1)S(1)} async-done(((bf16[64,2,512]{2,1,0:T(2,128)(2,1)}), bf16[64,2,512]{2,1,0:T(2,128)(2,1)S(1)}, u32[]{:S(2)}, u32[]{:S(2)}) %all-to-all-start.3) | async-done | bytes 131104 | tf_op jit(solution)/shard_map/all_to_all | solution.py:122
  120.4 0.7 bitcast_reduce_fusion
  121.3 0.7 copy.77
  121.9 240.2 %all-reduce.2.cloned.1.call-done = f32[2048,512]{1,0:T(8,128)} async-done(((f32[2048,512]{1,0:T(8,128)}), f32[2048,512]{1,0:T(8,128)}) %all-reduce.2.cloned.1.call-update) | async-done | bytes 4194320 | tf_op jit(solution)/shard_map/psum | solution.py:134
  362.1 1.5 dynamic-slice_multiply_fusion
  (84 shorter events, 8.6 us)
Async XLA Ops:
  7.2 56.8 %copy-start = (bf16[1536,512]{1,0:T(8,128)(2,1)S(1)}, bf16[1536,512]{1,0:T(8,128)(2,1)}, u32[]{:S(2)}) copy-start(bf16[1536,512]{1,0:T(8,128)(2,1)} %param.12) | copy-start | bytes 4718596
  10.5 33.5 %all-to-all-start = ((bf16[1,2,64,512]{3,1,0,2:T(2,128)(2,1)}), bf16[1,2,64,512]{3,1,0,2:T(2,128)(2,1)S(1)}, u32[]{:S(2)}, u32[]{:S(2)}) async-start(bf16[1,2,64,512]{3,1,0,2:T(2,128)(2,1)} %copy.63), calls=%async_computation | async-start | bytes 262144 | tf_op jit(solution)/shard_map/all_to_all | solution.py:44
  44.0 18.6 %all-to-all-start.1 = ((bf16[1,2,64,512]{3,1,0,2:T(2,128)(2,1)}), bf16[1,2,64,512]{3,1,0,2:T(2,128)(2,1)S(1)}, u32[]{:S(2)}, u32[]{:S(2)}) async-start(bf16[1,2,64,512]{3,1,0,2:T(2,128)(2,1)} %copy.67), calls=%async_computation.1 | async-start | bytes 262144 | tf_op jit(solution)/shard_map/all_to_all | solution.py:45
  48.6 313.5 %all-reduce.2.cloned.1.call-start = ((), (), s32[]{:S(2)}) async-start(), calls=%async_computation.4 | async-start | bytes 8388608 | tf_op jit(solution)/shard_map/psum | solution.py:134
  78.5 1.0 copy-start.1
  82.7 19.0 %all-to-all-start.2 = ((bf16[64,2,512]{2,1,0:T(2,128)(2,1)}), bf16[64,2,512]{2,1,0:T(2,128)(2,1)S(1)}, u32[]{:S(2)}, u32[]{:S(2)}) async-start(bf16[64,2,512]{2,1,0:T(2,128)(2,1)} %reshape.155), calls=%async_computation.2 | async-start | bytes 262144 | tf_op jit(solution)/shard_map/all_to_all | solution.py:121
  101.7 18.6 %all-to-all-start.3 = ((bf16[64,2,512]{2,1,0:T(2,128)(2,1)}), bf16[64,2,512]{2,1,0:T(2,128)(2,1)S(1)}, u32[]{:S(2)}, u32[]{:S(2)}) async-start(bf16[64,2,512]{2,1,0:T(2,128)(2,1)} %reshape.157), calls=%async_computation.3 | async-start | bytes 262144 | tf_op jit(solution)/shard_map/all_to_all | solution.py:122
Sparse Core Ops, SparseCore 0:
  78.7 283.3 all-reduce.1
where the time goes:
time: 372 us; the launch traced here: 370 us
  waiting for transfers between devices  289 us (78%)
  starting transfers between devices  33.4 us (9%)
  between operations  14.2 us (4%)
  matrix products  12.2 us (3%)
  other arithmetic  11.9 us (3%)
  local copies, waits for them, and re-layouts  9.88 us (3%)
    psum x1, waiting for transfers between devices, per_device(): summed_all = lax.psum(grad_term, ('grp', 'cell'))  240 us
    all_to_all x1, starting transfers between devices, per_device(): lax.all_to_all(shifted, 'cell', split_axis=2, concat_axis=1, tiled=True)  19.6 us
    all_to_all x1, waiting for transfers between devices, per_device(): lax.all_to_all(grad_in[None], 'cell', split_axis=1, concat_axis=2, tiled=...  12.4 us
    all_to_all x1, waiting for transfers between devices, per_device(): lax.all_to_all(shifted, 'cell', split_axis=2, concat_axis=1, tiled=True)  12.2 us
    all_to_all x1, waiting for transfers between devices, per_device(): lax.all_to_all(cotangent, 'cell', split_axis=2, concat_axis=1, tiled=True)  12.2 us
    all_to_all x1, waiting for transfers between devices, per_device(): lax.all_to_all(output[None], 'cell', split_axis=1, concat_axis=2, tiled=T...  11.6 us
  transfers between devices with their start and end apart: 5, of which 5 were waited for; matrix products, arithmetic and copies ran while one was open for 3% of the time, Pallas kernels for 0%

commit v1 on v0

v1 whole, which is shorter than its diff:
```python
import functools
import math

import jax
import jax.numpy as jnp
import numpy as np
from jax import lax
from jax.experimental import pallas as pl
from jax.experimental.pallas import tpu as pltpu
from jax.sharding import Mesh, PartitionSpec as P

HEADS = 8
BLK = 32
F32 = jnp.float32
BF16 = jnp.bfloat16
AXES = ("z_lo", "core", "x", "z_hi", "y")
GRP = ("z_lo", "core")
CELL = ("x", "z_hi", "y")
DEPTH = ("z_hi", "z_lo", "core")
LANES = 128
VMEM = pl.BlockSpec(memory_space=pltpu.VMEM)
SMEM = pl.BlockSpec(memory_space=pltpu.SMEM)


def call(body, out_shape, n_in, scratch=(), smem=(), name=None):
    multi = isinstance(out_shape, (tuple, list))
    return pl.pallas_call(
        body,
        out_shape=out_shape,
        in_specs=[SMEM if i in smem else VMEM for i in range(n_in)],
        out_specs=[VMEM] * len(out_shape) if multi else VMEM,
        scratch_shapes=list(scratch),
        name=name,
    )


def nt(a, b):
    return lax.dot_general(a, b, (((1,), (1,)), ((), ())), preferred_element_type=F32)


def nn(a, b):
    return jnp.dot(a, b, preferred_element_type=F32)


def put_chunks(scr, value, tensor):
    for r in range(2):
        for k in range(4):
            scr[pl.ds(tensor * 8 + r * 4 + k, 64, stride=16), :] = value[
                r * 64 : (r + 1) * 64, k * LANES : (k + 1) * LANES
            ]


def get_chunks(scr, tensor):
    return jnp.concatenate(
        [
            jnp.concatenate(
                [scr[pl.ds(tensor * 8 + r * 4 + k, 64, stride=16), :] for k in range(4)], axis=1
            )
            for r in range(2)
        ],
        axis=0,
    )


def pack_body(treat_rows, embed, cot, treat_vec, send, scr):
    first = lax.axis_index(CELL) * 2
    vec = treat_vec[...]
    shifted = jnp.concatenate(
        [
            embed[0, r].astype(F32) + treat_rows[0, first + r].astype(F32) * vec
            for r in range(2)
        ],
        axis=0,
    )
    put_chunks(scr, shifted, 0)
    put_chunks(scr, jnp.concatenate([cot[0, 0], cot[0, 1]], axis=0).astype(F32), 1)
    send[...] = scr[...].astype(BF16).reshape(64, 16, LANES)


def unpack_body(recv, out, grad_in, scr):
    scr[...] = recv[...].reshape(1024, LANES).astype(F32)
    for tensor, ref in ((0, out), (1, grad_in)):
        value = get_chunks(scr, tensor).astype(BF16)
        ref[0, 0] = value[:64]
        ref[0, 1] = value[64:]


def main_body(recv, w_qkv, w_out, bias, send, keep, rows_out, scr):
    width = w_out.shape[0]
    scale = 1.0 / math.sqrt(width // HEADS)
    scr[...] = recv[...].reshape(1024, LANES).astype(F32)
    shift = get_chunks(scr, 0)
    cot = get_chunks(scr, 1)
    shift_b = shift.astype(BF16)
    cot_b = cot.astype(BF16)
    wq = w_qkv[...]
    wo = w_out[...]
    projected = nt(shift_b, wq).astype(BF16)
    grad_att = nn(cot_b, wo).astype(BF16)
    first = lax.broadcasted_iota(jnp.int32, (128, LANES), 1) < LANES // 2
    zero = jnp.zeros((128, LANES), BF16)
    bias_one = bias[...]
    bias2 = jnp.concatenate([bias_one, bias_one], axis=1)

    def two_heads(slab):
        return jnp.concatenate([jnp.where(first, slab, zero), jnp.where(first, zero, slab)], axis=0)

    def flip(pair):
        return jnp.concatenate([pair[:, :LANES].T, pair[:, LANES:].T], axis=1)

    att, gq, gk, gv = [], [], [], []
    for p in range(width // LANES):
        lo = p * LANES
        q = projected[:, lo : lo + LANES]
        k = projected[:, width + lo : width + lo + LANES]
        v = projected[:, 2 * width + lo : 2 * width + lo + LANES]
        ga = grad_att[:, lo : lo + LANES]
        q2, k2, v2, ga2 = two_heads(q), two_heads(k), two_heads(v), two_heads(ga)
        score = nt(k, q2) + bias2
        grad_prob = nt(v, ga2)
        peak = jnp.max(score, axis=0, keepdims=True)
        exp_score = jnp.exp((score - peak) * scale)
        total = jnp.sum(exp_score, axis=0, keepdims=True)
        prob = exp_score * (1.0 / total)
        prob_b = prob.astype(BF16)
        delta = jnp.sum(prob * grad_prob, axis=0, keepdims=True)
        grad_score = (prob * (grad_prob - delta) * scale).astype(BF16)
        att.append(nn(flip(prob_b), v2).astype(BF16))
        gq.append(nn(flip(grad_score), k2).astype(BF16))
        gk.append(nn(grad_score, q2).astype(BF16))
        gv.append(nn(prob_b, ga2).astype(BF16))
    attended = jnp.concatenate(att, axis=1)
    grad_proj = gq + gk + gv

    mine = lax.axis_index("core") == 0
    tall = [part.T for part in grad_proj] + [
        cot_b[:, k * LANES : (k + 1) * LANES].T for k in range(width // LANES)
    ]
    for n, part in enumerate(tall):
        part = part.reshape(4, 2, 16, LANES)
        even = part[:, 0].reshape(64, LANES)
        odd = part[:, 1].reshape(64, LANES)
        keep[n * 64 : (n + 1) * 64, :] = jnp.where(mine, even, odd)
        send[n * 64 : (n + 1) * 64, :] = jnp.where(mine, odd, even)
    for k in range(width // LANES):
        send[1024 + k * 128 : 1024 + (k + 1) * 128, :] = shift_b[:, k * LANES : (k + 1) * LANES]
        send[1536 + k * 128 : 1536 + (k + 1) * 128, :] = att[k]

    put_chunks(scr, shift + nt(attended, wo), 0)
    put_chunks(scr, cot + nn(jnp.concatenate(grad_proj, axis=1), wq), 1)
    rows_out[...] = scr[...].astype(BF16).reshape(64, 16, LANES)


def weight_body(keep, own, other, partial):
    def tokens(base):
        return jnp.concatenate(
            [
                jnp.concatenate(
                    [ref[base + k * 128 : base + (k + 1) * 128, :] for k in range(4)], axis=1
                )
                for ref in (own, other)
            ],
            axis=0,
        )

    left = jnp.concatenate([keep[...], other[:1024, :]], axis=1)
    shift = tokens(1024)
    att = tokens(1536)
    for x in range(4):
        right = shift if x < 3 else att
        partial[x] = nn(left[x * 256 : (x + 1) * 256], right).astype(BF16)


def sum_x_body(parts, out):
    total = parts[0].astype(F32)
    for x in range(1, 4):
        total = total + parts[x].astype(F32)
    total = total.astype(BF16)
    for z in range(2):
        for y in range(8):
            out[y, z * 16 : (z + 1) * 16, :] = total[(z * 8 + y) * 16 : (z * 8 + y + 1) * 16]


def sum_y_body(parts, out):
    total = parts[0].astype(F32)
    for y in range(1, 8):
        total = total + parts[y].astype(F32)
    total = total.astype(BF16)
    for n in range(16):
        out[n] = total[:16] if n < 8 else total[16:]


def sum_z_body(gscale, parts, out):
    for core in range(2):
        total = parts[core].astype(F32)
        for z in range(1, 8):
            total = total + parts[2 * z + core].astype(F32)
        out[core * 16 : (core + 1) * 16, :] = total * gscale


def key_bias(is_train, pattern):
    train = jnp.transpose(is_train.reshape(64, 2)).reshape(128)
    block = np.tile(np.arange(64) // 16, 2)
    picked = (block[:, None] == np.arange(4)[None, :]).astype(np.float32)
    spread = jnp.einsum("jb,ab,ia->ji", picked, (pattern == 1).astype(F32), picked)
    allowed = ((spread > 0.5) & (train[:, None] == 1)) | np.eye(128, dtype=bool)
    return jnp.where(allowed, 0.0, -jnp.inf).astype(F32)


def per_device(row_embed, cotangent, w_qkv, w_out, treat_vec, is_train, treated, block_pattern):
    chunk = jax.ShapeDtypeStruct((64, 16, LANES), BF16)
    scr = pltpu.VMEM((1024, LANES), F32)
    rows = row_embed.shape
    packed = call(pack_body, chunk, 4, [scr], (0,), "pack")(
        treated, row_embed, cotangent, treat_vec.reshape(1, -1)
    )
    bias = key_bias(is_train[0], block_pattern)
    recv = lax.all_to_all(packed, CELL, 0, 0, tiled=True)
    send, keep, rows_out = call(
        main_body,
        [
            jax.ShapeDtypeStruct((2048, LANES), BF16),
            jax.ShapeDtypeStruct((1024, LANES), BF16),
            chunk,
        ],
        4,
        [scr],
        (),
        "attend",
    )(recv, w_qkv, w_out, bias)
    other = lax.ppermute(send, "core", [(0, 1), (1, 0)])
    partial = call(
        weight_body, jax.ShapeDtypeStruct((4, 256, 512), BF16), 3, name="weight"
    )(keep, send, other)
    by_x = lax.all_to_all(partial, "x", 0, 0, tiled=True)
    part_y = call(sum_x_body, jax.ShapeDtypeStruct((8, 32, 512), BF16), 1, name="sum_x")(by_x)
    by_y = lax.all_to_all(part_y, "y", 0, 0, tiled=True)
    part_z = call(sum_y_body, jax.ShapeDtypeStruct((16, 16, 512), BF16), 1, name="sum_y")(by_y)
    by_z = lax.all_to_all(part_z, DEPTH, 0, 0, tiled=True)
    gscale = 1.0 / math.sqrt(8 * 128 * 64)
    summed = call(
        functools.partial(sum_z_body, gscale),
        jax.ShapeDtypeStruct((32, 512), F32),
        1,
        name="sum_z",
    )(by_z)
    back = lax.all_to_all(rows_out, CELL, 0, 0, tiled=True)
    out, grad_in = call(
        unpack_body,
        [jax.ShapeDtypeStruct(rows, BF16), jax.ShapeDtypeStruct(rows, BF16)],
        1,
        [scr],
        name="unpack",
    )(back)
    return out, grad_in, summed


def solution(mesh):
    fine = Mesh(mesh.devices.reshape(4, 2, 4, 2, 8), AXES)
    cells = P(GRP, CELL, None, None)
    return jax.shard_map(
        per_device,
        mesh=fine,
        in_specs=(cells, cells, P(), P(), P(), P(GRP, None), P(GRP, None), P()),
        out_specs=(cells, cells, P(CELL, None)),
        check_vma=False,
    )
```

time: 372 us -> 132 us (0.35)
  waiting for transfers between devices: 289 us -> 37.5 us
  blocking collectives: 0 us -> 33.3 us
  Pallas kernels: 0 us -> 16.8 us
  between operations: 14.2 us -> 0.68 us
  other arithmetic: 11.9 us -> 0.68 us
  matrix products: 12.2 us -> 1.86 us
  local copies, waits for them, and re-layouts: 9.88 us -> 2.54 us
  starting transfers between devices: 33.4 us -> 37.5 us
    psum x1 -> x0, waiting for transfers between devices: 240 us -> none  [per_device(): summed_all = lax.psum(grad_term, ('grp', 'cell'))]
    all_to_all x0 -> x2, blocking collectives: none -> 33.3 us  [the longest x1 19.2 us: per_device(): by_x = lax.all_to_all(partial, 'x', 0, 0, tiled=True)]
    pallas_call x0 -> x7, Pallas kernels: none -> 16.8 us  [the longest x1 5.09 us: per_device(): call(main_body, [jax.ShapeDtypeStruct((2048, LANES), BF16), jax.ShapeDtyp...]
    all_to_all x4 -> x3, waiting for transfers between devices: 48.5 us -> 35.8 us  [the longest x1 13.3 us: per_device(): back = lax.all_to_all(rows_out, CELL, 0, 0, tiled=True)]
    dot_general x54 -> x1, matrix products: 12.2 us -> 1.86 us  [key_bias(): jnp.einsum('jb,ab,ia->ji', picked, (pattern == 1).astype(F32), picked)]
    ppermute x0 -> x1, starting transfers between devices: none -> 4.91 us  [per_device(): other = lax.ppermute(send, 'core', [(0, 1), (1, 0)])]
    unnamed x12 -> x8, local copies, waits for them, and re-layouts: 6.2 us -> 2.22 us
    all_to_all x4 -> x3, starting transfers between devices: 33.4 us -> 32.6 us  [the longest x1 19.6 us: per_device(): recv = lax.all_to_all(packed, CELL, 0, 0, tiled=True)]
  transfers between devices with their start and end apart: 5 -> 4, of which waited for: 5 -> 4; matrix products, arithmetic and copies ran while one was open for 3% -> 2% of each run, Pallas kernels for 0% -> 3%
where the time goes in v1:
time: 132 us; the launch traced here: 131 us
  starting transfers between devices  37.5 us (28%)
  waiting for transfers between devices  37.5 us (28%)
  blocking collectives  33.3 us (25%)
  Pallas kernels  16.8 us (13%)
  local copies, waits for them, and re-layouts  2.54 us (2%)
  matrix products  1.86 us (1%)
    all_to_all x1, starting transfers between devices, per_device(): recv = lax.all_to_all(packed, CELL, 0, 0, tiled=True)  19.6 us
    all_to_all x1, blocking collectives, per_device(): by_x = lax.all_to_all(partial, 'x', 0, 0, tiled=True)  19.2 us
    all_to_all x1, blocking collectives, per_device(): by_y = lax.all_to_all(part_y, 'y', 0, 0, tiled=True)  14.2 us
    all_to_all x1, waiting for transfers between devices, per_device(): back = lax.all_to_all(rows_out, CELL, 0, 0, tiled=True)  13.3 us
    all_to_all x1, waiting for transfers between devices, per_device(): recv = lax.all_to_all(packed, CELL, 0, 0, tiled=True)  12.6 us
    all_to_all x1, waiting for transfers between devices, per_device(): by_z = lax.all_to_all(part_z, DEPTH, 0, 0, tiled=True)  9.91 us
    all_to_all x1, starting transfers between devices, per_device(): by_z = lax.all_to_all(part_z, DEPTH, 0, 0, tiled=True)  8.43 us
    pallas_call x1, Pallas kernels, per_device(): call(main_body, [jax.ShapeDtypeStruct((2048, LANES), BF16), jax.ShapeDtyp...  5.09 us
  transfers between devices with their start and end apart: 4, of which 4 were waited for; matrix products, arithmetic and copies ran while one was open for 2% of the time, Pallas kernels for 3%

profile of v1, /device:TPU:1, one launch (start us, length us, event | category | flops | bytes accessed | tf_op | source)
XLA Modules:
  0.0 130.9 jit_solution(9012979038127812770)
XLA Ops:
  0.6 1.9 %pack.1 = bf16[64,16,128]{2,1,0:T(8,128)(2,1)} custom-call(s32[1,128]{1,0:T(1,128)} %treat_rows.1, bf16[1,2,64,512]{3,2,1,0:T(8,128)(2,1)} %embed.1, bf16[1,2,64,512]{3,2,1,0:T(8,128)(2,1)} %cot.1, f32[1,512]{1,0:T(1,128)} %bitcast.5), custom_call_target="tpu_custom_call" | custom-call | tf_op jit(solution)/shard_map/pack/pallas_call | solution.py:214
  2.5 19.6 %all-to-all-start = ((bf16[64,16,128]{2,1,0:T(8,128)(2,1)}), bf16[64,16,128]{2,1,0:T(8,128)(2,1)S(1)}, u32[]{:S(2)}, u32[]{:S(2)}) async-start(bf16[64,16,128]{2,1,0:T(8,128)(2,1)} %pack.1), calls=%async_computation | async-start | bytes 524288 | tf_op jit(solution)/shard_map/all_to_all | solution.py:218
  22.1 0.7 compare_reduce_fusion
  22.8 0.2 eq.26
  22.9 0.1 copy.15
  23.0 0.1 eq.28
  23.1 1.9 %fusion.2.bias = f32[128,128]{1,0:T(8,128)} fusion(pred[128,128]{1,0:T(32,128)(4,1)} %constant.14.clone, bf16[128,4]{1,0:T(8,128)(2,1)} %constant.27, pred[128]{0:T(512)(128)(4,1)S(1)} %eq.28, s32[4,4]{1,0:T(4,128)} %param.18), kind=kOutput, calls=%fused_computation.3 | convolution fusion | flops 200720 | bytes 83136 | tf_op jit(solution)/shard_map/jb,ab,ia->ji/dot_general | solution.py:205
  24.9 12.6 %all-to-all-done.recv = bf16[64,16,128]{2,1,0:T(8,128)(2,1)S(1)} async-done(((bf16[64,16,128]{2,1,0:T(8,128)(2,1)}), bf16[64,16,128]{2,1,0:T(8,128)(2,1)S(1)}, u32[]{:S(2)}, u32[]{:S(2)}) %all-to-all-start) | async-done | bytes 262176 | tf_op jit(solution)/shard_map/all_to_all | solution.py:218
  37.5 0.0 copy-start
  37.5 0.7 copy-done
  38.2 5.1 %attend.1 = (bf16[2048,128]{1,0:T(8,128)(2,1)}, bf16[1024,128]{1,0:T(8,128)(2,1)}, bf16[64,16,128]{2,1,0:T(8,128)(2,1)}) custom-call(bf16[64,16,128]{2,1,0:T(8,128)(2,1)} %copy-done, bf16[1536,512]{1,0:T(8,128)(2,1)} %w_qkv.1, bf16[512,512]{1,0:T(8,128)(2,1)} %w_out.1, f32[128,128]{1,0:T(8,128)} %fusion.2.bias), custom_call_target="tpu_custom_call" | custom-call | tf_op jit(solution)/shard_map/attend/pallas_call | solution.py:219
  43.3 4.9 %collective-permute-start = (bf16[2048,128]{1,0:T(8,128)(2,1)}, bf16[2048,128]{1,0:T(8,128)(2,1)S(1)}, u32[]{:S(2)}, u32[]{:S(2)}) collective-permute-start(bf16[2048,128]{1,0:T(8,128)(2,1)} %get-tuple-element.12.own), channel_id=1, source_target_pairs={{0,64},{64,0},{1,65},{65,1},{2,66},{66,2},{3,67},{67,3},{4,68},{68... | collective-permute-start | bytes 1572872 | tf_op jit(solution)/shard_map/ppermute | solution.py:231
  48.2 1.7 %collective-permute-done.other = bf16[2048,128]{1,0:T(8,128)(2,1)S(1)} collective-permute-done((bf16[2048,128]{1,0:T(8,128)(2,1)}, bf16[2048,128]{1,0:T(8,128)(2,1)S(1)}, u32[]{:S(2)}, u32[]{:S(2)}) %collective-permute-start) | collective-permute-done | bytes 524320 | tf_op jit(solution)/shard_map/ppermute | solution.py:231
  50.0 0.0 copy-start.3
  50.0 0.8 copy-done.3
  50.8 2.7 %weight.1 = bf16[4,256,512]{2,1,0:T(8,128)(2,1)} custom-call(bf16[1024,128]{1,0:T(8,128)(2,1)} %get-tuple-element.11.keep, bf16[2048,128]{1,0:T(8,128)(2,1)} %get-tuple-element.12.own, bf16[2048,128]{1,0:T(8,128)(2,1)} %copy-done.3), custom_call_target="tpu_custom_call" | custom-call | tf_op jit(solution)/shard_map/weight/pallas_call | solution.py:232
  53.5 19.2 %all_to_all.25.parts = bf16[4,256,512]{2,1,0:T(8,128)(2,1)} all-to-all(bf16[4,256,512]{2,1,0:T(8,128)(2,1)} %weight.1), channel_id=1, replica_groups=mesh['z_lo'=4,'core'=2,'x'=4,'z_hi'=2,'y'=8] {'x'}, dimensions={0} | all-to-all | bytes 2097152 | tf_op jit(solution)/shard_map/all_to_all | solution.py:235
  72.6 2.1 %sum_x.1 = bf16[8,32,512]{2,1,0:T(8,128)(2,1)} custom-call(bf16[4,256,512]{2,1,0:T(8,128)(2,1)} %all_to_all.25.parts), custom_call_target="tpu_custom_call" | custom-call | tf_op jit(solution)/shard_map/sum_x/pallas_call | solution.py:236
  74.7 14.2 %all_to_all.26.parts = bf16[8,32,512]{2,1,0:T(8,128)(2,1)} all-to-all(bf16[8,32,512]{2,1,0:T(8,128)(2,1)} %sum_x.1), channel_id=1, replica_groups=mesh['z_lo'=4,'core'=2,'x'=4,'z_hi'=2,'y'=8] {'y'}, dimensions={0} | all-to-all | bytes 524288 | tf_op jit(solution)/shard_map/all_to_all | solution.py:237
  88.8 4.6 %all-to-all-start.1 = ((bf16[64,16,128]{2,1,0:T(8,128)(2,1)}), bf16[64,16,128]{2,1,0:T(8,128)(2,1)S(1)}, u32[]{:S(2)}, u32[]{:S(2)}) async-start(bf16[64,16,128]{2,1,0:T(8,128)(2,1)} %get-tuple-element.8), calls=%async_computation.1 | async-start | bytes 524288 | tf_op jit(solution)/shard_map/all_to_all | solution.py:247
  93.5 1.7 %sum_y.1 = bf16[16,16,512]{2,1,0:T(8,128)(2,1)} custom-call(bf16[8,32,512]{2,1,0:T(8,128)(2,1)} %all_to_all.26.parts), custom_call_target="tpu_custom_call" | custom-call | tf_op jit(solution)/shard_map/sum_y/pallas_call | solution.py:238
  95.2 13.3 %all-to-all-done.1.recv = bf16[64,16,128]{2,1,0:T(8,128)(2,1)S(1)} async-done(((bf16[64,16,128]{2,1,0:T(8,128)(2,1)}), bf16[64,16,128]{2,1,0:T(8,128)(2,1)S(1)}, u32[]{:S(2)}, u32[]{:S(2)}) %all-to-all-start.1) | async-done | bytes 262176 | tf_op jit(solution)/shard_map/all_to_all | solution.py:247
  108.4 0.0 copy-start.2
  108.4 8.4 %all-to-all-start.4 = ((bf16[16,16,512]{2,1,0:T(8,128)(2,1)}), bf16[16,16,512]{2,1,0:T(8,128)(2,1)S(1)}, u32[]{:S(2)}, u32[]{:S(2)}) async-start(bf16[16,16,512]{2,1,0:T(8,128)(2,1)} %sum_y.1), calls=%async_computation.4 | async-start | bytes 524288 | tf_op jit(solution)/shard_map/all_to_all | solution.py:239
  116.9 0.0 copy-done.2
  116.9 1.8 %unpack.1 = (bf16[1,2,64,512]{3,2,1,0:T(8,128)(2,1)}, bf16[1,2,64,512]{3,2,1,0:T(8,128)(2,1)}) custom-call(bf16[64,16,128]{2,1,0:T(8,128)(2,1)} %copy-done.2), custom_call_target="tpu_custom_call" | custom-call | tf_op jit(solution)/shard_map/unpack/pallas_call | solution.py:248
  118.7 9.9 %all-to-all-done.4.parts = bf16[16,16,512]{2,1,0:T(8,128)(2,1)S(1)} async-done(((bf16[16,16,512]{2,1,0:T(8,128)(2,1)}), bf16[16,16,512]{2,1,0:T(8,128)(2,1)S(1)}, u32[]{:S(2)}, u32[]{:S(2)}) %all-to-all-start.4) | async-done | bytes 262176 | tf_op jit(solution)/shard_map/all_to_all | solution.py:239
  128.6 0.0 copy-start.1
  128.6 0.7 copy-done.1
  129.3 1.6 %sum_z.1 = f32[32,512]{1,0:T(8,128)} custom-call(bf16[16,16,512]{2,1,0:T(8,128)(2,1)} %copy-done.1), custom_call_target="tpu_custom_call" | custom-call | tf_op jit(solution)/shard_map/sum_z/pallas_call | solution.py:241
Async XLA Ops:
  2.5 35.0 %all-to-all-start = ((bf16[64,16,128]{2,1,0:T(8,128)(2,1)}), bf16[64,16,128]{2,1,0:T(8,128)(2,1)S(1)}, u32[]{:S(2)}, u32[]{:S(2)}) async-start(bf16[64,16,128]{2,1,0:T(8,128)(2,1)} %pack.1), calls=%async_computation | async-start | bytes 524288 | tf_op jit(solution)/shard_map/all_to_all | solution.py:218
  37.5 0.7 copy-start
  43.3 6.6 %collective-permute-start = (bf16[2048,128]{1,0:T(8,128)(2,1)}, bf16[2048,128]{1,0:T(8,128)(2,1)S(1)}, u32[]{:S(2)}, u32[]{:S(2)}) collective-permute-start(bf16[2048,128]{1,0:T(8,128)(2,1)} %get-tuple-element.12.own), channel_id=1, source_target_pairs={{0,64},{64,0},{1,65},{65,1},{2,66},{66,2},{3,67},{67,3},{4,68},{68... | collective-permute-start | bytes 1572872 | tf_op jit(solution)/shard_map/ppermute | solution.py:231
  50.0 0.8 copy-start.3
  88.8 19.6 %all-to-all-start.1 = ((bf16[64,16,128]{2,1,0:T(8,128)(2,1)}), bf16[64,16,128]{2,1,0:T(8,128)(2,1)S(1)}, u32[]{:S(2)}, u32[]{:S(2)}) async-start(bf16[64,16,128]{2,1,0:T(8,128)(2,1)} %get-tuple-element.8), calls=%async_computation.1 | async-start | bytes 524288 | tf_op jit(solution)/shard_map/all_to_all | solution.py:247
  108.4 8.4 %copy-start.2 = (bf16[64,16,128]{2,1,0:T(8,128)(2,1)}, bf16[64,16,128]{2,1,0:T(8,128)(2,1)S(1)}, u32[]{:S(2)}) copy-start(bf16[64,16,128]{2,1,0:T(8,128)(2,1)S(1)} %all-to-all-done.1.recv) | copy-start | bytes 786436
  108.4 20.1 %all-to-all-start.4 = ((bf16[16,16,512]{2,1,0:T(8,128)(2,1)}), bf16[16,16,512]{2,1,0:T(8,128)(2,1)S(1)}, u32[]{:S(2)}, u32[]{:S(2)}) async-start(bf16[16,16,512]{2,1,0:T(8,128)(2,1)} %sum_y.1), calls=%async_computation.4 | async-start | bytes 524288 | tf_op jit(solution)/shard_map/all_to_all | solution.py:239
  128.6 0.7 copy-start.1

commit v2 on v1

--- a/solution.py
+++ b/solution.py
@@ -3,7 +3,6 @@
 
 import jax
 import jax.numpy as jnp
-import numpy as np
 from jax import lax
 from jax.experimental import pallas as pl
 from jax.experimental.pallas import tpu as pltpu
@@ -22,16 +21,33 @@
 SMEM = pl.BlockSpec(memory_space=pltpu.SMEM)
 
 
-def call(body, out_shape, n_in, scratch=(), smem=(), name=None):
-    multi = isinstance(out_shape, (tuple, list))
-    return pl.pallas_call(
+def call(body, outs, n_in, scratch=(), smem=(), free=(), name=None):
+    run = pl.pallas_call(
         body,
-        out_shape=out_shape,
+        out_shape=[shape if keep_out else pltpu.VMEM(shape.shape, shape.dtype) for shape, keep_out in outs],
         in_specs=[SMEM if i in smem else VMEM for i in range(n_in)],
-        out_specs=[VMEM] * len(out_shape) if multi else VMEM,
+        out_specs=[VMEM] * len(outs),
         scratch_shapes=list(scratch),
         name=name,
     )
+
+    def apply(*args):
+        return run(
+            *[
+                a if i in smem or i in free else pltpu.with_memory_space_constraint(a, pltpu.VMEM)
+                for i, a in enumerate(args)
+            ]
+        )
+
+    return apply
+
+
+def held(*shape, dtype=BF16):
+    return (jax.ShapeDtypeStruct(shape, dtype), False)
+
+
+def given(shape, dtype):
+    return (jax.ShapeDtypeStruct(shape, dtype), True)
 
 
 def nt(a, b):
@@ -151,7 +167,7 @@
     rows_out[...] = scr[...].astype(BF16).reshape(64, 16, LANES)
 
 
-def weight_body(keep, own, other, partial):
+def weight_body(keep, own, other, *chunks):
     def tokens(base):
         return jnp.concatenate(
             [
@@ -163,18 +179,21 @@
             axis=0,
         )
 
-    left = jnp.concatenate([keep[...], other[:1024, :]], axis=1)
     shift = tokens(1024)
     att = tokens(1536)
-    for x in range(4):
-        right = shift if x < 3 else att
-        partial[x] = nn(left[x * 256 : (x + 1) * 256], right).astype(BF16)
-
-
-def sum_x_body(parts, out):
-    total = parts[0].astype(F32)
-    for x in range(1, 4):
-        total = total + parts[x].astype(F32)
+    x = lax.axis_index("x")
+    for d, chunk in enumerate(chunks):
+        place = lax.rem(x + d, 4)
+        here = pl.ds(pl.multiple_of(place * 256, 256), 256)
+        left = jnp.concatenate([keep[here, :], other[here, :]], axis=1)
+        right = jnp.where(place == 3, att, shift)
+        chunk[...] = nn(left, right).astype(BF16)
+
+
+def sum_x_body(own, a, b, c, after, out):
+    total = own[...].astype(F32)
+    for part in (a, b, c):
+        total = total + part[...].astype(F32)
     total = total.astype(BF16)
     for z in range(2):
         for y in range(8):
@@ -198,59 +217,61 @@
         out[core * 16 : (core + 1) * 16, :] = total * gscale
 
 
-def key_bias(is_train, pattern):
-    train = jnp.transpose(is_train.reshape(64, 2)).reshape(128)
-    block = np.tile(np.arange(64) // 16, 2)
-    picked = (block[:, None] == np.arange(4)[None, :]).astype(np.float32)
-    spread = jnp.einsum("jb,ab,ia->ji", picked, (pattern == 1).astype(F32), picked)
-    allowed = ((spread > 0.5) & (train[:, None] == 1)) | np.eye(128, dtype=bool)
-    return jnp.where(allowed, 0.0, -jnp.inf).astype(F32)
+def prep_body(pattern, train, w_qkv, w_out, bias, w_qkv_here, w_out_here):
+    key = lax.broadcasted_iota(jnp.int32, (128, 128), 0)
+    query = lax.broadcasted_iota(jnp.int32, (128, 128), 1)
+    key_block = lax.rem(key, 64) // 16
+    query_block = lax.rem(query, 64) // 16
+    open_block = jnp.zeros((128, 128), jnp.int32)
+    for a in range(4):
+        for b in range(4):
+            here = (query_block == a) & (key_block == b)
+            open_block = jnp.where(here, pattern[a, b], open_block)
+    allowed = ((open_block == 1) & (train[...] == 1)) | (key == query)
+    bias[...] = jnp.where(allowed, 0.0, -jnp.inf).astype(F32)
+    w_qkv_here[...] = w_qkv[...]
+    w_out_here[...] = w_out[...]
 
 
 def per_device(row_embed, cotangent, w_qkv, w_out, treat_vec, is_train, treated, block_pattern):
-    chunk = jax.ShapeDtypeStruct((64, 16, LANES), BF16)
     scr = pltpu.VMEM((1024, LANES), F32)
     rows = row_embed.shape
-    packed = call(pack_body, chunk, 4, [scr], (0,), "pack")(
+    (packed,) = call(pack_body, [held(64, 16, LANES)], 4, [scr], (0,), (1, 2, 3), "pack")(
         treated, row_embed, cotangent, treat_vec.reshape(1, -1)
     )
-    bias = key_bias(is_train[0], block_pattern)
+    train = jnp.transpose(is_train.reshape(64, 2)).reshape(128, 1)
+    bias, w_qkv, w_out = call(
+        prep_body,
+        [held(128, 128, dtype=F32), held(*w_qkv.shape), held(*w_out.shape)],
+        4,
+        smem=(0,),
+        free=(1, 2, 3),
+        name="prep",
+    )(block_pattern, train, w_qkv, w_out)
     recv = lax.all_to_all(packed, CELL, 0, 0, tiled=True)
     send, keep, rows_out = call(
         main_body,
-        [
-            jax.ShapeDtypeStruct((2048, LANES), BF16),
-            jax.ShapeDtypeStruct((1024, LANES), BF16),
-            chunk,
-        ],
+        [held(2048, LANES), held(1024, LANES), held(64, 16, LANES)],
         4,
         [scr],
-        (),
-        "attend",
+        name="attend",
     )(recv, w_qkv, w_out, bias)
     other = lax.ppermute(send, "core", [(0, 1), (1, 0)])
-    partial = call(
-        weight_body, jax.ShapeDtypeStruct((4, 256, 512), BF16), 3, name="weight"
-    )(keep, send, other)
-    by_x = lax.all_to_all(partial, "x", 0, 0, tiled=True)
-    part_y = call(sum_x_body, jax.ShapeDtypeStruct((8, 32, 512), BF16), 1, name="sum_x")(by_x)
+    chunks = call(weight_body, [held(256, 512)] * 4, 3, name="weight")(keep, send, other)
+    by_x = [chunks[0]] + [
+        lax.ppermute(chunks[d], "x", [(i, (i + d) % 4) for i in range(4)]) for d in (2, 1, 3)
+    ]
+    back = lax.all_to_all(rows_out, CELL, 0, 0, tiled=True)
+    (part_y,) = call(sum_x_body, [held(8, 32, 512)], 5, name="sum_x")(*by_x, back)
     by_y = lax.all_to_all(part_y, "y", 0, 0, tiled=True)
-    part_z = call(sum_y_body, jax.ShapeDtypeStruct((16, 16, 512), BF16), 1, name="sum_y")(by_y)
+    (part_z,) = call(sum_y_body, [held(16, 16, 512)], 1, name="sum_y")(by_y)
     by_z = lax.all_to_all(part_z, DEPTH, 0, 0, tiled=True)
     gscale = 1.0 / math.sqrt(8 * 128 * 64)
-    summed = call(
-        functools.partial(sum_z_body, gscale),
-        jax.ShapeDtypeStruct((32, 512), F32),
-        1,
-        name="sum_z",
+    (summed,) = call(
+        functools.partial(sum_z_body, gscale), [given((32, 512), F32)], 1, name="sum_z"
     )(by_z)
-    back = lax.all_to_all(rows_out, CELL, 0, 0, tiled=True)
     out, grad_in = call(
-        unpack_body,
-        [jax.ShapeDtypeStruct(rows, BF16), jax.ShapeDtypeStruct(rows, BF16)],
-        1,
-        [scr],
-        name="unpack",
+        unpack_body, [given(rows, BF16), given(rows, BF16)], 1, [scr], name="unpack"
     )(back)
     return out, grad_in, summed
 

time: 132 us -> 111 us (0.84)
  blocking collectives: 33.3 us -> 16.4 us
  starting transfers between devices: 37.5 us -> 47.7 us
  waiting for transfers between devices: 37.5 us -> 30 us
  Pallas kernels: 16.8 us -> 10.8 us
  matrix products: 1.86 us -> 0 us
    all_to_all x1 -> x0, blocking collectives: 19.2 us -> none  [per_device(): by_x = lax.all_to_all(partial, 'x', 0, 0, tiled=True)]
    ppermute x0 -> x3, starting transfers between devices: none -> 11 us  [per_device(): lax.ppermute(chunks[d], 'x', [(i, (i + d) % 4) for i in range(4)])]
    all_to_all x1, waiting for transfers between devices: 13.3 us -> 3.17 us  [per_device(): back = lax.all_to_all(rows_out, CELL, 0, 0, tiled=True)]
    pallas_call x7 -> x8, Pallas kernels: 16.8 us -> 10.8 us  [apply(): run(*[a if i in smem or i in free else pltpu.with_memory_space_constraint...]
    ppermute x0 -> x3, waiting for transfers between devices: none -> 5.01 us  [per_device(): lax.ppermute(chunks[d], 'x', [(i, (i + d) % 4) for i in range(4)])]
    all_to_all x1, blocking collectives: 14.2 us -> 16.4 us  [per_device(): by_y = lax.all_to_all(part_y, 'y', 0, 0, tiled=True)]
    dot_general x1 -> x0, matrix products: 1.86 us -> none  [key_bias(): jnp.einsum('jb,ab,ia->ji', picked, (pattern == 1).astype(F32), picked)]
    ppermute x1, waiting for transfers between devices: 1.73 us -> 0.01 us  [per_device(): other = lax.ppermute(send, 'core', [(0, 1), (1, 0)])]
  transfers between devices with their start and end apart: 4 -> 7, of which waited for: 4 -> 4; matrix products, arithmetic and copies ran while one was open for 2% -> 3% of each run, Pallas kernels for 3% -> 4%
where the time goes in v2:
time: 111 us; the launch traced here: 110 us
  starting transfers between devices  47.7 us (43%)
  waiting for transfers between devices  30 us (27%)
  blocking collectives  16.4 us (15%)
  Pallas kernels  10.8 us (10%)
  local copies, waits for them, and re-layouts  3.16 us (3%)
  other arithmetic  1.32 us (1%)
    all_to_all x1, starting transfers between devices, per_device(): recv = lax.all_to_all(packed, CELL, 0, 0, tiled=True)  19.6 us
    all_to_all x1, blocking collectives, per_device(): by_y = lax.all_to_all(part_y, 'y', 0, 0, tiled=True)  16.4 us
    ppermute x3, starting transfers between devices, per_device(): lax.ppermute(chunks[d], 'x', [(i, (i + d) % 4) for i in range(4)])  11 us
    all_to_all x1, waiting for transfers between devices, per_device(): recv = lax.all_to_all(packed, CELL, 0, 0, tiled=True)  10.9 us
    all_to_all x1, waiting for transfers between devices, per_device(): by_z = lax.all_to_all(part_z, DEPTH, 0, 0, tiled=True)  10.9 us
    pallas_call x8, Pallas kernels, apply(): run(*[a if i in smem or i in free else pltpu.with_memory_space_constraint...  10.8 us
    all_to_all x1, starting transfers between devices, per_device(): by_z = lax.all_to_all(part_z, DEPTH, 0, 0, tiled=True)  7.64 us
    ppermute x3, waiting for transfers between devices, per_device(): lax.ppermute(chunks[d], 'x', [(i, (i + d) % 4) for i in range(4)])  5.01 us
  transfers between devices with their start and end apart: 7, of which 4 were waited for; matrix products, arithmetic and copies ran while one was open for 3% of the time, Pallas kernels for 4%

profile of v2, /device:TPU:1, one launch (start us, length us, event | category | flops | bytes accessed | tf_op | source)
XLA Modules:
  0.0 110.2 jit_solution(11625696092715200657)
XLA Ops:
  0.6 1.9 %pack.1 = bf16[64,16,128]{2,1,0:T(8,128)(2,1)} custom-call(s32[1,128]{1,0:T(1,128)} %treat_rows.1, bf16[1,2,64,512]{3,2,1,0:T(8,128)(2,1)} %embed.1, bf16[1,2,64,512]{3,2,1,0:T(8,128)(2,1)} %cot.1, f32[1,512]{1,0:T(1,128)} %bitcast.3), custom_call_target="tpu_custom_call" | custom-call | tf_op jit(solution)/shard_map/pack/pallas_call | solution.py:35
  2.5 19.6 %all-to-all-start = ((bf16[64,16,128]{2,1,0:T(8,128)(2,1)}), bf16[64,16,128]{2,1,0:T(8,128)(2,1)S(1)}, u32[]{:S(2)}, u32[]{:S(2)}) async-start(bf16[64,16,128]{2,1,0:T(8,128)(2,1)} %pack.1), calls=%async_computation | async-start | bytes 524288 | tf_op jit(solution)/shard_map/all_to_all | solution.py:251
  22.1 0.5 broadcast.3
  22.6 1.3 %reduce.3 = s32[128]{0:T(128)S(1)} reduce(s32[1,128]{1,0:T(1,128)} %param.13, s32[]{:T(128)} %broadcast.3), dimensions={0}, to_apply=%param.13.reduce_sub_computation.3 | reduce | bytes 1028 | tf_op args[5]
  23.9 0.1 reshape.16
  24.0 0.1 copy.13
  24.1 0.8 reshape.18.train
  24.9 1.7 %prep.1 = (f32[128,128]{1,0:T(8,128)S(1)}, bf16[1536,512]{1,0:T(8,128)(2,1)S(1)}, bf16[512,512]{1,0:T(8,128)(2,1)S(1)}) custom-call(s32[4,4]{1,0:T(4,128)} %pattern.1, s32[128,1]{1,0:T(8,128)} %reshape.18.train, bf16[1536,512]{1,0:T(8,128)(2,1)} %w_qkv.1, bf16[512,512]{1,0:T(8,128)(2,1)} %w_out.1), custom_call_target="tpu_custom_call" | custom-call | tf_op jit(solution)/shard_map/prep/pallas_call | solution.py:35
  26.6 10.9 %all-to-all-done.recv = bf16[64,16,128]{2,1,0:T(8,128)(2,1)S(1)} async-done(((bf16[64,16,128]{2,1,0:T(8,128)(2,1)}), bf16[64,16,128]{2,1,0:T(8,128)(2,1)S(1)}, u32[]{:S(2)}, u32[]{:S(2)}) %all-to-all-start) | async-done | bytes 262176 | tf_op jit(solution)/shard_map/all_to_all | solution.py:251
  37.5 3.4 %attend.1 = (bf16[2048,128]{1,0:T(8,128)(2,1)}, bf16[1024,128]{1,0:T(8,128)(2,1)S(1)}, bf16[64,16,128]{2,1,0:T(8,128)(2,1)}) custom-call(bf16[64,16,128]{2,1,0:T(8,128)(2,1)S(1)} %all-to-all-done.recv, bf16[1536,512]{1,0:T(8,128)(2,1)S(1)} %get-tuple-element.15.w_qkv, bf16[512,512]{1,0:T(8,128)(2,1)S(1)} %get-tuple-element.16.w_out, ...), custom_call_target="tpu_custom_call" | custom-call | tf_op jit(solution)/shard_map/attend/pallas_call | solution.py:35
  40.9 0.0 copy-start
  40.9 0.7 copy-done
  41.6 4.9 %collective-permute-start = (bf16[2048,128]{1,0:T(8,128)(2,1)}, bf16[2048,128]{1,0:T(8,128)(2,1)S(1)}, u32[]{:S(2)}, u32[]{:S(2)}) collective-permute-start(bf16[2048,128]{1,0:T(8,128)(2,1)} %get-tuple-element.22.own), channel_id=1, source_target_pairs={{0,64},{64,0},{1,65},{65,1},{2,66},{66,2},{3,67},{67,3},{4,68},{68... | collective-permute-start | bytes 1572872 | tf_op jit(solution)/shard_map/ppermute | solution.py:259
  46.5 4.6 %all-to-all-start.1 = ((bf16[64,16,128]{2,1,0:T(8,128)(2,1)}), bf16[64,16,128]{2,1,0:T(8,128)(2,1)S(1)}, u32[]{:S(2)}, u32[]{:S(2)}) async-start(bf16[64,16,128]{2,1,0:T(8,128)(2,1)} %get-tuple-element.18), calls=%async_computation.1 | async-start | bytes 524288 | tf_op jit(solution)/shard_map/all_to_all | solution.py:264
  51.2 0.0 collective-permute-done.other
  51.2 0.0 copy-start.1
  51.2 0.9 copy-done.1
  52.1 1.5 %weight.1 = (bf16[256,512]{1,0:T(8,128)(2,1)S(1)}, bf16[256,512]{1,0:T(8,128)(2,1)S(1)}, bf16[256,512]{1,0:T(8,128)(2,1)S(1)}, bf16[256,512]{1,0:T(8,128)(2,1)S(1)}) custom-call(bf16[1024,128]{1,0:T(8,128)(2,1)S(1)} %copy-done.1, bf16[2048,128]{1,0:T(8,128)(2,1)} %get-tuple-element.22.own, bf16[2048,128]{1,0:T(8,128)(2,1)S(1)} %collective-permute-done.other), custom_call_target="tpu_custom_call" | custom-call | tf_op jit(solution)/shard_map/weight/pallas_call | solution.py:35
  53.6 4.5 %collective-permute-start.1 = (bf16[256,512]{1,0:T(8,128)(2,1)S(1)}, bf16[256,512]{1,0:T(8,128)(2,1)S(1)}, u32[]{:S(2)}, u32[]{:S(2)}) collective-permute-start(bf16[256,512]{1,0:T(8,128)(2,1)S(1)} %get-tuple-element.24), channel_id=1, source_target_pairs={{0,32},{16,48},{32,0},{48,16},{1,33},{17,49},{33,1},{49,17},{2,34}... | collective-permute-start | bytes 786440 | tf_op jit(solution)/shard_map/ppermute | solution.py:262
  58.2 2.3 %collective-permute-start.2 = (bf16[256,512]{1,0:T(8,128)(2,1)S(1)}, bf16[256,512]{1,0:T(8,128)(2,1)S(1)}, u32[]{:S(2)}, u32[]{:S(2)}) collective-permute-start(bf16[256,512]{1,0:T(8,128)(2,1)S(1)} %get-tuple-element.25), channel_id=1, source_target_pairs={{0,16},{16,32},{32,48},{48,0},{1,17},{17,33},{33,49},{49,1},{2,18}... | collective-permute-start | bytes 786440 | tf_op jit(solution)/shard_map/ppermute | solution.py:262
  60.5 4.2 %collective-permute-start.3 = (bf16[256,512]{1,0:T(8,128)(2,1)S(1)}, bf16[256,512]{1,0:T(8,128)(2,1)S(1)}, u32[]{:S(2)}, u32[]{:S(2)}) collective-permute-start(bf16[256,512]{1,0:T(8,128)(2,1)S(1)} %get-tuple-element.26), channel_id=1, source_target_pairs={{0,48},{16,0},{32,16},{48,32},{1,49},{17,1},{33,17},{49,33},{2,50}... | collective-permute-start | bytes 786440 | tf_op jit(solution)/shard_map/ppermute | solution.py:262
  64.7 3.2 %all-to-all-done.1.recv.after = bf16[64,16,128]{2,1,0:T(8,128)(2,1)S(1)} async-done(((bf16[64,16,128]{2,1,0:T(8,128)(2,1)}), bf16[64,16,128]{2,1,0:T(8,128)(2,1)S(1)}, u32[]{:S(2)}, u32[]{:S(2)}) %all-to-all-start.1) | async-done | bytes 262176 | tf_op jit(solution)/shard_map/all_to_all | solution.py:264
  67.8 0.0 collective-permute-done.1.a
  67.8 5.0 %collective-permute-done.2.b = bf16[256,512]{1,0:T(8,128)(2,1)S(1)} collective-permute-done((bf16[256,512]{1,0:T(8,128)(2,1)S(1)}, bf16[256,512]{1,0:T(8,128)(2,1)S(1)}, u32[]{:S(2)}, u32[]{:S(2)}) %collective-permute-start.2) | collective-permute-done | bytes 262176 | tf_op jit(solution)/shard_map/ppermute | solution.py:262
  72.8 0.0 collective-permute-done.3.c
  72.8 0.1 sum_x.1
  73.0 16.4 %all_to_all.20.parts = bf16[8,32,512]{2,1,0:T(8,128)(2,1)S(1)} all-to-all(bf16[8,32,512]{2,1,0:T(8,128)(2,1)S(1)} %sum_x.1), channel_id=1, replica_groups=mesh['z_lo'=4,'core'=2,'x'=4,'z_hi'=2,'y'=8] {'y'}, dimensions={0} | all-to-all | bytes 524288 | tf_op jit(solution)/shard_map/all_to_all | solution.py:266
  89.4 0.7 sum_y.1
  90.2 7.6 %all-to-all-start.3 = ((bf16[16,16,512]{2,1,0:T(8,128)(2,1)}), bf16[16,16,512]{2,1,0:T(8,128)(2,1)S(1)}, u32[]{:S(2)}, u32[]{:S(2)}) async-start(bf16[16,16,512]{2,1,0:T(8,128)(2,1)} %sum_y.1), calls=%async_computation.3 | async-start | bytes 524288 | tf_op jit(solution)/shard_map/all_to_all | solution.py:268
  97.8 0.8 unpack.1
  98.6 10.9 %all-to-all-done.3.parts = bf16[16,16,512]{2,1,0:T(8,128)(2,1)S(1)} async-done(((bf16[16,16,512]{2,1,0:T(8,128)(2,1)}), bf16[16,16,512]{2,1,0:T(8,128)(2,1)S(1)}, u32[]{:S(2)}, u32[]{:S(2)}) %all-to-all-start.3) | async-done | bytes 262176 | tf_op jit(solution)/shard_map/all_to_all | solution.py:268
  109.5 0.7 sum_z.1
Async XLA Ops:
  2.5 35.0 %all-to-all-start = ((bf16[64,16,128]{2,1,0:T(8,128)(2,1)}), bf16[64,16,128]{2,1,0:T(8,128)(2,1)S(1)}, u32[]{:S(2)}, u32[]{:S(2)}) async-start(bf16[64,16,128]{2,1,0:T(8,128)(2,1)} %pack.1), calls=%async_computation | async-start | bytes 524288 | tf_op jit(solution)/shard_map/all_to_all | solution.py:251
  40.9 0.7 copy-start
  41.6 9.5 %collective-permute-start = (bf16[2048,128]{1,0:T(8,128)(2,1)}, bf16[2048,128]{1,0:T(8,128)(2,1)S(1)}, u32[]{:S(2)}, u32[]{:S(2)}) collective-permute-start(bf16[2048,128]{1,0:T(8,128)(2,1)} %get-tuple-element.22.own), channel_id=1, source_target_pairs={{0,64},{64,0},{1,65},{65,1},{2,66},{66,2},{3,67},{67,3},{4,68},{68... | collective-permute-start | bytes 1572872 | tf_op jit(solution)/shard_map/ppermute | solution.py:259
  46.5 21.3 %all-to-all-start.1 = ((bf16[64,16,128]{2,1,0:T(8,128)(2,1)}), bf16[64,16,128]{2,1,0:T(8,128)(2,1)S(1)}, u32[]{:S(2)}, u32[]{:S(2)}) async-start(bf16[64,16,128]{2,1,0:T(8,128)(2,1)} %get-tuple-element.18), calls=%async_computation.1 | async-start | bytes 524288 | tf_op jit(solution)/shard_map/all_to_all | solution.py:264
  51.2 1.0 copy-start.1
  53.6 14.2 %collective-permute-start.1 = (bf16[256,512]{1,0:T(8,128)(2,1)S(1)}, bf16[256,512]{1,0:T(8,128)(2,1)S(1)}, u32[]{:S(2)}, u32[]{:S(2)}) collective-permute-start(bf16[256,512]{1,0:T(8,128)(2,1)S(1)} %get-tuple-element.24), channel_id=1, source_target_pairs={{0,32},{16,48},{32,0},{48,16},{1,33},{17,49},{33,1},{49,17},{2,34}... | collective-permute-start | bytes 786440 | tf_op jit(solution)/shard_map/ppermute | solution.py:262
  58.2 14.7 %collective-permute-start.2 = (bf16[256,512]{1,0:T(8,128)(2,1)S(1)}, bf16[256,512]{1,0:T(8,128)(2,1)S(1)}, u32[]{:S(2)}, u32[]{:S(2)}) collective-permute-start(bf16[256,512]{1,0:T(8,128)(2,1)S(1)} %get-tuple-element.25), channel_id=1, source_target_pairs={{0,16},{16,32},{32,48},{48,0},{1,17},{17,33},{33,49},{49,1},{2,18}... | collective-permute-start | bytes 786440 | tf_op jit(solution)/shard_map/ppermute | solution.py:262
  60.5 12.4 %collective-permute-start.3 = (bf16[256,512]{1,0:T(8,128)(2,1)S(1)}, bf16[256,512]{1,0:T(8,128)(2,1)S(1)}, u32[]{:S(2)}, u32[]{:S(2)}) collective-permute-start(bf16[256,512]{1,0:T(8,128)(2,1)S(1)} %get-tuple-element.26), channel_id=1, source_target_pairs={{0,48},{16,0},{32,16},{48,32},{1,49},{17,1},{33,17},{49,33},{2,50}... | collective-permute-start | bytes 786440 | tf_op jit(solution)/shard_map/ppermute | solution.py:262
  90.2 19.3 %all-to-all-start.3 = ((bf16[16,16,512]{2,1,0:T(8,128)(2,1)}), bf16[16,16,512]{2,1,0:T(8,128)(2,1)S(1)}, u32[]{:S(2)}, u32[]{:S(2)}) async-start(bf16[16,16,512]{2,1,0:T(8,128)(2,1)} %sum_y.1), calls=%async_computation.3 | async-start | bytes 524288 | tf_op jit(solution)/shard_map/all_to_all | solution.py:268

commit v3 on v2

--- a/solution.py
+++ b/solution.py
@@ -15,7 +15,7 @@
 AXES = ("z_lo", "core", "x", "z_hi", "y")
 GRP = ("z_lo", "core")
 CELL = ("x", "z_hi", "y")
-DEPTH = ("z_hi", "z_lo", "core")
+ROWS = ("z_hi", "y")
 LANES = 128
 VMEM = pl.BlockSpec(memory_space=pltpu.VMEM)
 SMEM = pl.BlockSpec(memory_space=pltpu.SMEM)
@@ -28,6 +28,7 @@
         in_specs=[SMEM if i in smem else VMEM for i in range(n_in)],
         out_specs=[VMEM] * len(outs),
         scratch_shapes=list(scratch),
+        compiler_params=None if free else pltpu.CompilerParams(vmem_limit_bytes=16 * 2**20),
         name=name,
     )
 
@@ -93,12 +94,16 @@
     send[...] = scr[...].astype(BF16).reshape(64, 16, LANES)
 
 
-def unpack_body(recv, out, grad_in, scr):
-    scr[...] = recv[...].reshape(1024, LANES).astype(F32)
-    for tensor, ref in ((0, out), (1, grad_in)):
-        value = get_chunks(scr, tensor).astype(BF16)
-        ref[0, 0] = value[:64]
-        ref[0, 1] = value[64:]
+def unpack_body(recv, out, grad_in, *scr):
+    for k, part in enumerate(scr):
+        lanes = slice(k * LANES, (k + 1) * LANES)
+        part[...] = recv[:, 16:, lanes].astype(F32).reshape(256, LANES)
+        for x in range(4):
+            for n, ref in enumerate((out, grad_in)):
+                for r in range(2):
+                    ref[0, r, x * 16 : (x + 1) * 16, lanes] = part[
+                        pl.ds(x * 4 + 2 * n + r, 16, stride=16), :
+                    ].astype(BF16)
 
 
 def main_body(recv, w_qkv, w_out, bias, send, keep, rows_out, scr):
@@ -162,12 +167,17 @@
         send[1024 + k * 128 : 1024 + (k + 1) * 128, :] = shift_b[:, k * LANES : (k + 1) * LANES]
         send[1536 + k * 128 : 1536 + (k + 1) * 128, :] = att[k]
 
-    put_chunks(scr, shift + nt(attended, wo), 0)
-    put_chunks(scr, cot + nn(jnp.concatenate(grad_proj, axis=1), wq), 1)
-    rows_out[...] = scr[...].astype(BF16).reshape(64, 16, LANES)
-
-
-def weight_body(keep, own, other, *chunks):
+    out = (shift + nt(attended, wo)).astype(BF16)
+    grad_in = (cot + nn(jnp.concatenate(grad_proj, axis=1), wq)).astype(BF16)
+    for x in range(4):
+        for n, value in enumerate((out, grad_in)):
+            for r in range(2):
+                rows_out[x, (2 * n + r) * 16 : (2 * n + r + 1) * 16, :] = value[
+                    r * 64 + x * 16 : r * 64 + (x + 1) * 16
+                ]
+
+
+def weight_body(keep, own, other, rows_out, merged):
     def tokens(base):
         return jnp.concatenate(
             [
@@ -179,40 +189,43 @@
             axis=0,
         )
 
+    left = jnp.concatenate([keep[...], other[:1024, :]], axis=1)
     shift = tokens(1024)
     att = tokens(1536)
-    x = lax.axis_index("x")
-    for d, chunk in enumerate(chunks):
-        place = lax.rem(x + d, 4)
-        here = pl.ds(pl.multiple_of(place * 256, 256), 256)
-        left = jnp.concatenate([keep[here, :], other[here, :]], axis=1)
-        right = jnp.where(place == 3, att, shift)
-        chunk[...] = nn(left, right).astype(BF16)
-
-
-def sum_x_body(own, a, b, c, after, out):
-    total = own[...].astype(F32)
-    for part in (a, b, c):
-        total = total + part[...].astype(F32)
+    for x in range(4):
+        right = shift if x < 3 else att
+        merged[x, :256, :] = nn(left[x * 256 : (x + 1) * 256], right).astype(BF16)
+        merged[x, 256:, :] = rows_out[x]
+
+
+def sum_x_body(parts, out, *scr):
+    total = parts[0, :256].astype(F32)
+    for x in range(1, 4):
+        total = total + parts[x, :256].astype(F32)
+    out[:, :16, :] = total.astype(BF16).reshape(16, 16, 512)
+    for k, part in enumerate(scr):
+        lanes = slice(k * LANES, (k + 1) * LANES)
+        for x in range(4):
+            for m in range(4):
+                part[pl.ds(x * 4 + m, 16, stride=16), :] = parts[
+                    x, 256 + m * 16 : 256 + (m + 1) * 16, lanes
+                ].astype(F32)
+        out[:, 16:, lanes] = part[...].astype(BF16).reshape(16, 16, LANES)
+
+
+def sum_rows_body(parts, out):
+    total = parts[0, :16].astype(F32)
+    for n in range(1, 16):
+        total = total + parts[n, :16].astype(F32)
     total = total.astype(BF16)
-    for z in range(2):
-        for y in range(8):
-            out[y, z * 16 : (z + 1) * 16, :] = total[(z * 8 + y) * 16 : (z * 8 + y + 1) * 16]
-
-
-def sum_y_body(parts, out):
-    total = parts[0].astype(F32)
-    for y in range(1, 8):
-        total = total + parts[y].astype(F32)
-    total = total.astype(BF16)
-    for n in range(16):
-        out[n] = total[:16] if n < 8 else total[16:]
+    for n in range(8):
+        out[n] = total
 
 
 def sum_z_body(gscale, parts, out):
     for core in range(2):
         total = parts[core].astype(F32)
-        for z in range(1, 8):
+        for z in range(1, 4):
             total = total + parts[2 * z + core].astype(F32)
         out[core * 16 : (core + 1) * 16, :] = total * gscale
 
@@ -251,28 +264,28 @@
     recv = lax.all_to_all(packed, CELL, 0, 0, tiled=True)
     send, keep, rows_out = call(
         main_body,
-        [held(2048, LANES), held(1024, LANES), held(64, 16, LANES)],
+        [held(2048, LANES), held(1024, LANES), held(4, 64, 512)],
         4,
         [scr],
         name="attend",
     )(recv, w_qkv, w_out, bias)
     other = lax.ppermute(send, "core", [(0, 1), (1, 0)])
-    chunks = call(weight_body, [held(256, 512)] * 4, 3, name="weight")(keep, send, other)
-    by_x = [chunks[0]] + [
-        lax.ppermute(chunks[d], "x", [(i, (i + d) % 4) for i in range(4)]) for d in (2, 1, 3)
-    ]
-    back = lax.all_to_all(rows_out, CELL, 0, 0, tiled=True)
-    (part_y,) = call(sum_x_body, [held(8, 32, 512)], 5, name="sum_x")(*by_x, back)
-    by_y = lax.all_to_all(part_y, "y", 0, 0, tiled=True)
-    (part_z,) = call(sum_y_body, [held(16, 16, 512)], 1, name="sum_y")(by_y)
-    by_z = lax.all_to_all(part_z, DEPTH, 0, 0, tiled=True)
+    (merged,) = call(weight_body, [held(4, 320, 512)], 4, name="weight")(
+        keep, send, other, rows_out
+    )
+    by_x = lax.all_to_all(merged, "x", 0, 0, tiled=True)
+    tall = [pltpu.VMEM((256, LANES), F32)] * 4
+    (part_rows,) = call(sum_x_body, [held(16, 32, 512)], 1, tall, name="sum_x")(by_x)
+    by_rows = lax.all_to_all(part_rows, ROWS, 0, 0, tiled=True)
+    (part_z,) = call(sum_rows_body, [held(8, 16, 512)], 1, name="sum_rows")(by_rows)
+    by_z = lax.all_to_all(part_z, GRP, 0, 0, tiled=True)
     gscale = 1.0 / math.sqrt(8 * 128 * 64)
     (summed,) = call(
         functools.partial(sum_z_body, gscale), [given((32, 512), F32)], 1, name="sum_z"
     )(by_z)
     out, grad_in = call(
-        unpack_body, [given(rows, BF16), given(rows, BF16)], 1, [scr], name="unpack"
-    )(back)
+        unpack_body, [given(rows, BF16), given(rows, BF16)], 1, tall, name="unpack"
+    )(by_rows)
     return out, grad_in, summed
 
 

time: 111 us -> 103 us (0.928)
  blocking collectives: 16.4 us -> 39.7 us
  starting transfers between devices: 47.7 us -> 32.4 us
  waiting for transfers between devices: 30 us -> 17.4 us
  Pallas kernels: 10.8 us -> 9.14 us
  local copies, waits for them, and re-layouts: 3.16 us -> 1.5 us
    all_to_all x1 -> x2, blocking collectives: 16.4 us -> 39.7 us  [the longest x1 20.1 us: per_device(): by_x = lax.all_to_all(merged, 'x', 0, 0, tiled=True)]
    ppermute x3 -> x0, starting transfers between devices: 11 us -> none  [per_device(): lax.ppermute(chunks[d], 'x', [(i, (i + d) % 4) for i in range(4)])]
    all_to_all x2 -> x1, waiting for transfers between devices: 14 us -> 4.92 us  [per_device(): by_z = lax.all_to_all(part_z, GRP, 0, 0, tiled=True)]
    ppermute x3 -> x0, waiting for transfers between devices: 5.01 us -> none  [per_device(): lax.ppermute(chunks[d], 'x', [(i, (i + d) % 4) for i in range(4)])]
    all_to_all x2 -> x1, starting transfers between devices: 12.2 us -> 7.87 us  [per_device(): by_z = lax.all_to_all(part_z, GRP, 0, 0, tiled=True)]
    pallas_call x8, Pallas kernels: 10.8 us -> 9.14 us  [apply(): run(*[a if i in smem or i in free else pltpu.with_memory_space_constraint...]
    unnamed x5 -> x1, local copies, waits for them, and re-layouts: 2.17 us -> 0.51 us
    ppermute x1, waiting for transfers between devices: 0.01 us -> 1.51 us  [per_device(): other = lax.ppermute(send, 'core', [(0, 1), (1, 0)])]
  transfers between devices with their start and end apart: 7 -> 3, of which waited for: 4 -> 3; matrix products, arithmetic and copies ran while one was open for 3% -> 3% of each run, Pallas kernels for 4% -> 3%
where the time goes in v3:
time: 103 us; the launch traced here: 102 us
  blocking collectives  39.7 us (39%)
  starting transfers between devices  32.4 us (31%)
  waiting for transfers between devices  17.4 us (17%)
  Pallas kernels  9.14 us (9%)
  local copies, waits for them, and re-layouts  1.5 us (1%)
  other arithmetic  1.32 us (1%)
    all_to_all x1, blocking collectives, per_device(): by_x = lax.all_to_all(merged, 'x', 0, 0, tiled=True)  20.1 us
    all_to_all x1, blocking collectives, per_device(): by_rows = lax.all_to_all(part_rows, ROWS, 0, 0, tiled=True)  19.6 us
    all_to_all x1, starting transfers between devices, per_device(): recv = lax.all_to_all(packed, CELL, 0, 0, tiled=True)  19.6 us
    all_to_all x1, waiting for transfers between devices, per_device(): recv = lax.all_to_all(packed, CELL, 0, 0, tiled=True)  10.9 us
    pallas_call x8, Pallas kernels, apply(): run(*[a if i in smem or i in free else pltpu.with_memory_space_constraint...  9.14 us
    all_to_all x1, starting transfers between devices, per_device(): by_z = lax.all_to_all(part_z, GRP, 0, 0, tiled=True)  7.87 us
    ppermute x1, starting transfers between devices, per_device(): other = lax.ppermute(send, 'core', [(0, 1), (1, 0)])  4.92 us
    all_to_all x1, waiting for transfers between devices, per_device(): by_z = lax.all_to_all(part_z, GRP, 0, 0, tiled=True)  4.92 us
  transfers between devices with their start and end apart: 3, of which 3 were waited for; matrix products, arithmetic and copies ran while one was open for 3% of the time, Pallas kernels for 3%

profile of v3, /device:TPU:1, one launch (start us, length us, event | category | flops | bytes accessed | tf_op | source)
XLA Modules:
  0.0 102.1 jit_solution(2690037251341456326)
XLA Ops:
  0.6 1.9 %pack.1 = bf16[64,16,128]{2,1,0:T(8,128)(2,1)} custom-call(s32[1,128]{1,0:T(1,128)} %treat_rows.1, bf16[1,2,64,512]{3,2,1,0:T(8,128)(2,1)} %embed.1, bf16[1,2,64,512]{3,2,1,0:T(8,128)(2,1)} %cot.1, f32[1,512]{1,0:T(1,128)} %bitcast.3), custom_call_target="tpu_custom_call" | custom-call | tf_op jit(solution)/shard_map/pack/pallas_call | solution.py:36
  2.5 19.6 %all-to-all-start = ((bf16[64,16,128]{2,1,0:T(8,128)(2,1)}), bf16[64,16,128]{2,1,0:T(8,128)(2,1)S(1)}, u32[]{:S(2)}, u32[]{:S(2)}) async-start(bf16[64,16,128]{2,1,0:T(8,128)(2,1)} %pack.1), calls=%async_computation | async-start | bytes 524288 | tf_op jit(solution)/shard_map/all_to_all | solution.py:264
  22.1 0.5 broadcast.3
  22.6 1.3 %reduce.3 = s32[128]{0:T(128)S(1)} reduce(s32[1,128]{1,0:T(1,128)} %param.13, s32[]{:T(128)} %broadcast.3), dimensions={0}, to_apply=%param.13.reduce_sub_computation.3 | reduce | bytes 1028 | tf_op args[5]
  23.9 0.1 reshape.16
  24.0 0.1 copy.13
  24.1 0.8 reshape.18.train
  24.9 1.7 %prep.1 = (f32[128,128]{1,0:T(8,128)S(1)}, bf16[1536,512]{1,0:T(8,128)(2,1)S(1)}, bf16[512,512]{1,0:T(8,128)(2,1)S(1)}) custom-call(s32[4,4]{1,0:T(4,128)} %pattern.1, s32[128,1]{1,0:T(8,128)} %reshape.18.train, bf16[1536,512]{1,0:T(8,128)(2,1)} %w_qkv.1, bf16[512,512]{1,0:T(8,128)(2,1)} %w_out.1), custom_call_target="tpu_custom_call" | custom-call | tf_op jit(solution)/shard_map/prep/pallas_call | solution.py:36
  26.6 10.9 %all-to-all-done.recv = bf16[64,16,128]{2,1,0:T(8,128)(2,1)S(1)} async-done(((bf16[64,16,128]{2,1,0:T(8,128)(2,1)}), bf16[64,16,128]{2,1,0:T(8,128)(2,1)S(1)}, u32[]{:S(2)}, u32[]{:S(2)}) %all-to-all-start) | async-done | bytes 262176 | tf_op jit(solution)/shard_map/all_to_all | solution.py:264
  37.5 2.5 %attend.1 = (bf16[2048,128]{1,0:T(8,128)(2,1)S(1)}, bf16[1024,128]{1,0:T(8,128)(2,1)S(1)}, bf16[4,64,512]{2,1,0:T(8,128)(2,1)S(1)}) custom-call(bf16[64,16,128]{2,1,0:T(8,128)(2,1)S(1)} %all-to-all-done.recv, bf16[1536,512]{1,0:T(8,128)(2,1)S(1)} %get-tuple-element.11.w_qkv, bf16[512,512]{1,0:T(8,128)(2,1)S(1)} %get-tuple-element.12.w_out, ...), custom_call_target="tpu_custom_call" | custom-call | tf_op jit(solution)/shard_map/attend/pallas_call | solution.py:36
  40.0 4.9 %collective-permute-start = (bf16[2048,128]{1,0:T(8,128)(2,1)S(1)}, bf16[2048,128]{1,0:T(8,128)(2,1)S(1)}, u32[]{:S(2)}, u32[]{:S(2)}) collective-permute-start(bf16[2048,128]{1,0:T(8,128)(2,1)S(1)} %get-tuple-element.15.own), channel_id=1, source_target_pairs={{0,64},{64,0},{1,65},{65,1},{2,66},{66,2},{3,67},{67,3},{4,68},{68... | collective-permute-start | bytes 1572872 | tf_op jit(solution)/shard_map/ppermute | solution.py:272
  45.0 1.5 %collective-permute-done.other = bf16[2048,128]{1,0:T(8,128)(2,1)S(1)} collective-permute-done((bf16[2048,128]{1,0:T(8,128)(2,1)S(1)}, bf16[2048,128]{1,0:T(8,128)(2,1)S(1)}, u32[]{:S(2)}, u32[]{:S(2)}) %collective-permute-start) | collective-permute-done | bytes 524320 | tf_op jit(solution)/shard_map/ppermute | solution.py:272
  46.5 0.4 weight.1
  46.9 20.1 %all_to_all.20.parts = bf16[4,320,512]{2,1,0:T(8,128)(2,1)S(1)} all-to-all(bf16[4,320,512]{2,1,0:T(8,128)(2,1)S(1)} %weight.1), channel_id=1, replica_groups=mesh['z_lo'=4,'core'=2,'x'=4,'z_hi'=2,'y'=8] {'x'}, dimensions={0} | all-to-all | bytes 2621440 | tf_op jit(solution)/shard_map/all_to_all | solution.py:276
  67.0 0.4 sum_x.1
  67.4 19.6 %all_to_all.21.recv.parts = bf16[16,32,512]{2,1,0:T(8,128)(2,1)S(1)} all-to-all(bf16[16,32,512]{2,1,0:T(8,128)(2,1)S(1)} %sum_x.1), channel_id=1, replica_groups=mesh['z_lo'=4,'core'=2,'x'=4,'z_hi'=2,'y'=8] {'z_hi','y'}, dimensions={0} | all-to-all | bytes 1048576 | tf_op jit(solution)/shard_map/all_to_all | solution.py:279
  87.1 0.7 sum_rows.1
  87.8 7.9 %all-to-all-start.3 = ((bf16[8,16,512]{2,1,0:T(8,128)(2,1)}), bf16[8,16,512]{2,1,0:T(8,128)(2,1)S(1)}, u32[]{:S(2)}, u32[]{:S(2)}) async-start(bf16[8,16,512]{2,1,0:T(8,128)(2,1)} %sum_rows.1), calls=%async_computation.3 | async-start | bytes 262144 | tf_op jit(solution)/shard_map/all_to_all | solution.py:281
  95.6 0.9 unpack.1
  96.5 4.9 %all-to-all-done.3.parts = bf16[8,16,512]{2,1,0:T(8,128)(2,1)S(1)} async-done(((bf16[8,16,512]{2,1,0:T(8,128)(2,1)}), bf16[8,16,512]{2,1,0:T(8,128)(2,1)S(1)}, u32[]{:S(2)}, u32[]{:S(2)}) %all-to-all-start.3) | async-done | bytes 131104 | tf_op jit(solution)/shard_map/all_to_all | solution.py:281
  101.4 0.7 sum_z.1
Async XLA Ops:
  2.5 35.0 %all-to-all-start = ((bf16[64,16,128]{2,1,0:T(8,128)(2,1)}), bf16[64,16,128]{2,1,0:T(8,128)(2,1)S(1)}, u32[]{:S(2)}, u32[]{:S(2)}) async-start(bf16[64,16,128]{2,1,0:T(8,128)(2,1)} %pack.1), calls=%async_computation | async-start | bytes 524288 | tf_op jit(solution)/shard_map/all_to_all | solution.py:264
  40.0 6.4 %collective-permute-start = (bf16[2048,128]{1,0:T(8,128)(2,1)S(1)}, bf16[2048,128]{1,0:T(8,128)(2,1)S(1)}, u32[]{:S(2)}, u32[]{:S(2)}) collective-permute-start(bf16[2048,128]{1,0:T(8,128)(2,1)S(1)} %get-tuple-element.15.own), channel_id=1, source_target_pairs={{0,64},{64,0},{1,65},{65,1},{2,66},{66,2},{3,67},{67,3},{4,68},{68... | collective-permute-start | bytes 1572872 | tf_op jit(solution)/shard_map/ppermute | solution.py:272
  87.8 13.7 %all-to-all-start.3 = ((bf16[8,16,512]{2,1,0:T(8,128)(2,1)}), bf16[8,16,512]{2,1,0:T(8,128)(2,1)S(1)}, u32[]{:S(2)}, u32[]{:S(2)}) async-start(bf16[8,16,512]{2,1,0:T(8,128)(2,1)} %sum_rows.1), calls=%async_computation.3 | async-start | bytes 262144 | tf_op jit(solution)/shard_map/all_to_all | solution.py:281

commit v4 on v3

--- a/solution.py
+++ b/solution.py
@@ -12,10 +12,11 @@
 BLK = 32
 F32 = jnp.float32
 BF16 = jnp.bfloat16
-AXES = ("z_lo", "core", "x", "z_hi", "y")
+AXES = ("z_lo", "core", "x", "z_hi", "y_hi", "y_lo")
 GRP = ("z_lo", "core")
-CELL = ("x", "z_hi", "y")
-ROWS = ("z_hi", "y")
+CELL = ("x", "z_hi", "y_hi", "y_lo")
+NEAR = ("x", "y_lo")
+FAR = ("z_hi", "y_hi")
 LANES = 128
 VMEM = pl.BlockSpec(memory_space=pltpu.VMEM)
 SMEM = pl.BlockSpec(memory_space=pltpu.SMEM)
@@ -95,18 +96,22 @@
 
 
 def unpack_body(recv, out, grad_in, *scr):
-    for k, part in enumerate(scr):
+    for k in range(4):
         lanes = slice(k * LANES, (k + 1) * LANES)
+        part, flat = scr[k], scr[4 + k]
         part[...] = recv[:, 16:, lanes].astype(F32).reshape(256, LANES)
         for x in range(4):
-            for n, ref in enumerate((out, grad_in)):
-                for r in range(2):
-                    ref[0, r, x * 16 : (x + 1) * 16, lanes] = part[
-                        pl.ds(x * 4 + 2 * n + r, 16, stride=16), :
-                    ].astype(BF16)
-
-
-def main_body(recv, w_qkv, w_out, bias, send, keep, rows_out, scr):
+            for y in range(2):
+                for m in range(4):
+                    flat[pl.ds(m * 64 + x * 16 + y, 8, stride=2), :] = part[
+                        pl.ds((2 * x + y) * 4 + m, 8, stride=32), :
+                    ]
+        for m in range(4):
+            ref = out if m < 2 else grad_in
+            ref[0, m % 2, :, lanes] = flat[m * 64 : (m + 1) * 64, :].astype(BF16)
+
+
+def main_body(recv, w_qkv, w_out, bias, send, keep, grads, scr):
     width = w_out.shape[0]
     scale = 1.0 / math.sqrt(width // HEADS)
     scr[...] = recv[...].reshape(1024, LANES).astype(F32)
@@ -150,7 +155,6 @@
         gq.append(nn(flip(grad_score), k2).astype(BF16))
         gk.append(nn(grad_score, q2).astype(BF16))
         gv.append(nn(prob_b, ga2).astype(BF16))
-    attended = jnp.concatenate(att, axis=1)
     grad_proj = gq + gk + gv
 
     mine = lax.axis_index("core") == 0
@@ -167,14 +171,31 @@
         send[1024 + k * 128 : 1024 + (k + 1) * 128, :] = shift_b[:, k * LANES : (k + 1) * LANES]
         send[1536 + k * 128 : 1536 + (k + 1) * 128, :] = att[k]
 
-    out = (shift + nt(attended, wo)).astype(BF16)
-    grad_in = (cot + nn(jnp.concatenate(grad_proj, axis=1), wq)).astype(BF16)
-    for x in range(4):
-        for n, value in enumerate((out, grad_in)):
-            for r in range(2):
-                rows_out[x, (2 * n + r) * 16 : (2 * n + r + 1) * 16, :] = value[
-                    r * 64 + x * 16 : r * 64 + (x + 1) * 16
-                ]
+    for p, part in enumerate(grad_proj):
+        grads[:, p * LANES : (p + 1) * LANES] = part
+
+
+def rows_body(recv, own, grads, w_qkv, w_out, rows_out, scr):
+    width = w_out.shape[0]
+    scr[...] = recv[...].reshape(1024, LANES).astype(F32)
+    shift = get_chunks(scr, 0)
+    cot = get_chunks(scr, 1)
+    attended = jnp.concatenate(
+        [own[1536 + k * 128 : 1536 + (k + 1) * 128, :] for k in range(width // LANES)], axis=1
+    )
+    out = shift + nt(attended, w_out[...])
+    grad_in = cot + nn(grads[...], w_qkv[...])
+    for k in range(width // LANES):
+        lanes = slice(k * LANES, (k + 1) * LANES)
+        here = scr.at[k * 256 : (k + 1) * 256]
+        here[:128, :] = out[:, lanes]
+        here[128:, :] = grad_in[:, lanes]
+        for x in range(4):
+            for y in range(2):
+                for m in range(4):
+                    rows_out[2 * x + y, m * 8 : (m + 1) * 8, lanes] = here[
+                        pl.ds(m * 64 + x * 16 + y, 8, stride=2), :
+                    ].astype(BF16)
 
 
 def weight_body(keep, own, other, rows_out, merged):
@@ -194,28 +215,30 @@
     att = tokens(1536)
     for x in range(4):
         right = shift if x < 3 else att
-        merged[x, :256, :] = nn(left[x * 256 : (x + 1) * 256], right).astype(BF16)
-        merged[x, 256:, :] = rows_out[x]
-
-
-def sum_x_body(parts, out, *scr):
-    total = parts[0, :256].astype(F32)
-    for x in range(1, 4):
-        total = total + parts[x, :256].astype(F32)
-    out[:, :16, :] = total.astype(BF16).reshape(16, 16, 512)
+        block = nn(left[x * 256 : (x + 1) * 256], right).astype(BF16).reshape(8, 2, 16, 512)
+        for y in range(2):
+            merged[2 * x + y, :128, :] = block[:, y].reshape(128, 512)
+            merged[2 * x + y, 128:, :] = rows_out[2 * x + y]
+
+
+def sum_near_body(parts, out, *scr):
+    total = parts[0, :128].astype(F32)
+    for n in range(1, 8):
+        total = total + parts[n, :128].astype(F32)
+    out[:, :16, :] = total.astype(BF16).reshape(8, 16, 512)
     for k, part in enumerate(scr):
         lanes = slice(k * LANES, (k + 1) * LANES)
-        for x in range(4):
+        for n in range(8):
             for m in range(4):
-                part[pl.ds(x * 4 + m, 16, stride=16), :] = parts[
-                    x, 256 + m * 16 : 256 + (m + 1) * 16, lanes
+                part[pl.ds(n * 4 + m, 8, stride=32), :] = parts[
+                    n, 128 + m * 8 : 128 + (m + 1) * 8, lanes
                 ].astype(F32)
-        out[:, 16:, lanes] = part[...].astype(BF16).reshape(16, 16, LANES)
-
-
-def sum_rows_body(parts, out):
+        out[:, 16:, lanes] = part[...].astype(BF16).reshape(8, 32, LANES)
+
+
+def sum_far_body(parts, out):
     total = parts[0, :16].astype(F32)
-    for n in range(1, 16):
+    for n in range(1, 8):
         total = total + parts[n, :16].astype(F32)
     total = total.astype(BF16)
     for n in range(8):
@@ -262,35 +285,38 @@
         name="prep",
     )(block_pattern, train, w_qkv, w_out)
     recv = lax.all_to_all(packed, CELL, 0, 0, tiled=True)
-    send, keep, rows_out = call(
+    send, keep, grads = call(
         main_body,
-        [held(2048, LANES), held(1024, LANES), held(4, 64, 512)],
+        [held(2048, LANES), held(1024, LANES), held(128, 1536)],
         4,
         [scr],
         name="attend",
     )(recv, w_qkv, w_out, bias)
     other = lax.ppermute(send, "core", [(0, 1), (1, 0)])
-    (merged,) = call(weight_body, [held(4, 320, 512)], 4, name="weight")(
+    (rows_out,) = call(rows_body, [held(8, 32, 512)], 5, [scr], name="rows")(
+        recv, send, grads, w_qkv, w_out
+    )
+    (merged,) = call(weight_body, [held(8, 160, 512)], 4, name="weight")(
         keep, send, other, rows_out
     )
-    by_x = lax.all_to_all(merged, "x", 0, 0, tiled=True)
+    by_near = lax.all_to_all(merged, NEAR, 0, 0, tiled=True)
     tall = [pltpu.VMEM((256, LANES), F32)] * 4
-    (part_rows,) = call(sum_x_body, [held(16, 32, 512)], 1, tall, name="sum_x")(by_x)
-    by_rows = lax.all_to_all(part_rows, ROWS, 0, 0, tiled=True)
-    (part_z,) = call(sum_rows_body, [held(8, 16, 512)], 1, name="sum_rows")(by_rows)
-    by_z = lax.all_to_all(part_z, GRP, 0, 0, tiled=True)
+    (part_near,) = call(sum_near_body, [held(8, 48, 512)], 1, tall, name="sum_near")(by_near)
+    by_far = lax.all_to_all(part_near, FAR, 0, 0, tiled=True)
+    (part_far,) = call(sum_far_body, [held(8, 16, 512)], 1, name="sum_far")(by_far)
+    by_z = lax.all_to_all(part_far, GRP, 0, 0, tiled=True)
     gscale = 1.0 / math.sqrt(8 * 128 * 64)
     (summed,) = call(
         functools.partial(sum_z_body, gscale), [given((32, 512), F32)], 1, name="sum_z"
     )(by_z)
     out, grad_in = call(
-        unpack_body, [given(rows, BF16), given(rows, BF16)], 1, tall, name="unpack"
-    )(by_rows)
+        unpack_body, [given(rows, BF16), given(rows, BF16)], 1, tall * 2, name="unpack"
+    )(by_far)
     return out, grad_in, summed
 
 
 def solution(mesh):
-    fine = Mesh(mesh.devices.reshape(4, 2, 4, 2, 8), AXES)
+    fine = Mesh(mesh.devices.reshape(4, 2, 4, 2, 4, 2), AXES)
     cells = P(GRP, CELL, None, None)
     return jax.shard_map(
         per_device,

time: 103 us -> 102 us (level)
  blocking collectives: 39.7 us -> 38.2 us
    all_to_all x2, blocking collectives: 39.7 us -> 38.2 us  [the longest x1 20.7 us: per_device(): by_near = lax.all_to_all(merged, NEAR, 0, 0, tiled=True)]
    pallas_call x8 -> x9, Pallas kernels: 9.14 us -> 9.76 us  [apply(): run(*[a if i in smem or i in free else pltpu.with_memory_space_constraint...]
where the time goes in v4:
time: 102 us; the launch traced here: 101 us
  blocking collectives  38.2 us (37%)
  starting transfers between devices  33.1 us (32%)
  waiting for transfers between devices  16.5 us (16%)
  Pallas kernels  9.76 us (10%)
  local copies, waits for them, and re-layouts  1.5 us (1%)
  other arithmetic  1.32 us (1%)
    all_to_all x1, blocking collectives, per_device(): by_near = lax.all_to_all(merged, NEAR, 0, 0, tiled=True)  20.7 us
    all_to_all x1, starting transfers between devices, per_device(): recv = lax.all_to_all(packed, CELL, 0, 0, tiled=True)  19.6 us
    all_to_all x1, blocking collectives, per_device(): by_far = lax.all_to_all(part_near, FAR, 0, 0, tiled=True)  17.6 us
    all_to_all x1, waiting for transfers between devices, per_device(): recv = lax.all_to_all(packed, CELL, 0, 0, tiled=True)  10.9 us
    pallas_call x9, Pallas kernels, apply(): run(*[a if i in smem or i in free else pltpu.with_memory_space_constraint...  9.76 us
    all_to_all x1, starting transfers between devices, per_device(): by_z = lax.all_to_all(part_far, GRP, 0, 0, tiled=True)  8.61 us
    ppermute x1, starting transfers between devices, per_device(): other = lax.ppermute(send, 'core', [(0, 1), (1, 0)])  4.93 us
    all_to_all x1, waiting for transfers between devices, per_device(): by_z = lax.all_to_all(part_far, GRP, 0, 0, tiled=True)  4.73 us
  transfers between devices with their start and end apart: 3, of which 3 were waited for; matrix products, arithmetic and copies ran while one was open for 3% of the time, Pallas kernels for 3%

profile of v4, /device:TPU:1, one launch (start us, length us, event | category | flops | bytes accessed | tf_op | source)
XLA Modules:
  0.0 101.2 jit_solution(9425491038485168415)
XLA Ops:
  0.6 1.9 %pack.1 = bf16[64,16,128]{2,1,0:T(8,128)(2,1)} custom-call(s32[1,128]{1,0:T(1,128)} %treat_rows.1, bf16[1,2,64,512]{3,2,1,0:T(8,128)(2,1)} %embed.1, bf16[1,2,64,512]{3,2,1,0:T(8,128)(2,1)} %cot.1, f32[1,512]{1,0:T(1,128)} %bitcast.3), custom_call_target="tpu_custom_call" | custom-call | tf_op jit(solution)/shard_map/pack/pallas_call | solution.py:37
  2.5 19.6 %all-to-all-start = ((bf16[64,16,128]{2,1,0:T(8,128)(2,1)}), bf16[64,16,128]{2,1,0:T(8,128)(2,1)S(1)}, u32[]{:S(2)}, u32[]{:S(2)}) async-start(bf16[64,16,128]{2,1,0:T(8,128)(2,1)} %pack.1), calls=%async_computation | async-start | bytes 524288 | tf_op jit(solution)/shard_map/all_to_all | solution.py:287
  22.1 0.5 broadcast.3
  22.6 1.3 %reduce.3 = s32[128]{0:T(128)S(1)} reduce(s32[1,128]{1,0:T(1,128)} %param.13, s32[]{:T(128)} %broadcast.3), dimensions={0}, to_apply=%param.13.reduce_sub_computation.3 | reduce | bytes 1028 | tf_op args[5]
  23.9 0.1 reshape.16
  24.0 0.1 copy.13
  24.1 0.8 reshape.18.train
  24.9 1.7 %prep.1 = (f32[128,128]{1,0:T(8,128)S(1)}, bf16[1536,512]{1,0:T(8,128)(2,1)S(1)}, bf16[512,512]{1,0:T(8,128)(2,1)S(1)}) custom-call(s32[4,4]{1,0:T(4,128)} %pattern.1, s32[128,1]{1,0:T(8,128)} %reshape.18.train, bf16[1536,512]{1,0:T(8,128)(2,1)} %w_qkv.1, bf16[512,512]{1,0:T(8,128)(2,1)} %w_out.1), custom_call_target="tpu_custom_call" | custom-call | tf_op jit(solution)/shard_map/prep/pallas_call | solution.py:37
  26.6 10.9 %all-to-all-done.recv = bf16[64,16,128]{2,1,0:T(8,128)(2,1)S(1)} async-done(((bf16[64,16,128]{2,1,0:T(8,128)(2,1)}), bf16[64,16,128]{2,1,0:T(8,128)(2,1)S(1)}, u32[]{:S(2)}, u32[]{:S(2)}) %all-to-all-start) | async-done | bytes 262176 | tf_op jit(solution)/shard_map/all_to_all | solution.py:287
  37.5 2.2 %attend.1 = (bf16[2048,128]{1,0:T(8,128)(2,1)S(1)}, bf16[1024,128]{1,0:T(8,128)(2,1)S(1)}, bf16[128,1536]{1,0:T(8,128)(2,1)S(1)}) custom-call(bf16[64,16,128]{2,1,0:T(8,128)(2,1)S(1)} %all-to-all-done.recv, bf16[1536,512]{1,0:T(8,128)(2,1)S(1)} %get-tuple-element.11.w_qkv, bf16[512,512]{1,0:T(8,128)(2,1)S(1)} %get-tuple-element.12.w_out, ...), custom_call_target="tpu_custom_call" | custom-call | tf_op jit(solution)/shard_map/attend/pallas_call | solution.py:37
  39.7 4.9 %collective-permute-start = (bf16[2048,128]{1,0:T(8,128)(2,1)S(1)}, bf16[2048,128]{1,0:T(8,128)(2,1)S(1)}, u32[]{:S(2)}, u32[]{:S(2)}) collective-permute-start(bf16[2048,128]{1,0:T(8,128)(2,1)S(1)} %get-tuple-element.15.own), channel_id=1, source_target_pairs={{0,64},{64,0},{1,65},{65,1},{2,66},{66,2},{3,67},{67,3},{4,68},{68... | collective-permute-start | bytes 1572872 | tf_op jit(solution)/shard_map/ppermute | solution.py:295
  44.7 0.6 rows.1.rows_out
  45.3 0.9 collective-permute-done.other
  46.2 0.4 weight.1
  46.6 20.7 %all_to_all.20.parts = bf16[8,160,512]{2,1,0:T(8,128)(2,1)S(1)} all-to-all(bf16[8,160,512]{2,1,0:T(8,128)(2,1)S(1)} %weight.1), channel_id=1, replica_groups=mesh['z_lo'=4,'core'=2,'x'=4,'z_hi'=2,'y_hi'=4,'y_lo'=2] {'x','y_lo'}, dimensions={0} | all-to-all | bytes 2621440 | tf_op jit(solution)/shard_map/all_to_all | solution.py:302
  67.3 0.5 sum_near.1
  67.9 17.6 %all_to_all.21.recv.parts = bf16[8,48,512]{2,1,0:T(8,128)(2,1)S(1)} all-to-all(bf16[8,48,512]{2,1,0:T(8,128)(2,1)S(1)} %sum_near.1), channel_id=1, replica_groups=mesh['z_lo'=4,'core'=2,'x'=4,'z_hi'=2,'y_hi'=4,'y_lo'=2] {'z_hi','y_hi'}, dimensions={0} | all-to-all | bytes 786432 | tf_op jit(solution)/shard_map/all_to_all | solution.py:305
  85.4 0.7 sum_far.1
  86.1 8.6 %all-to-all-start.3 = ((bf16[8,16,512]{2,1,0:T(8,128)(2,1)}), bf16[8,16,512]{2,1,0:T(8,128)(2,1)S(1)}, u32[]{:S(2)}, u32[]{:S(2)}) async-start(bf16[8,16,512]{2,1,0:T(8,128)(2,1)} %sum_far.1), calls=%async_computation.3 | async-start | bytes 262144 | tf_op jit(solution)/shard_map/all_to_all | solution.py:307
  94.7 1.1 %unpack.1 = (bf16[1,2,64,512]{3,2,1,0:T(8,128)(2,1)}, bf16[1,2,64,512]{3,2,1,0:T(8,128)(2,1)}) custom-call(bf16[8,48,512]{2,1,0:T(8,128)(2,1)S(1)} %all_to_all.21.recv.parts), custom_call_target="tpu_custom_call" | custom-call | tf_op jit(solution)/shard_map/unpack/pallas_call | solution.py:37
  95.8 4.7 %all-to-all-done.3.parts = bf16[8,16,512]{2,1,0:T(8,128)(2,1)S(1)} async-done(((bf16[8,16,512]{2,1,0:T(8,128)(2,1)}), bf16[8,16,512]{2,1,0:T(8,128)(2,1)S(1)}, u32[]{:S(2)}, u32[]{:S(2)}) %all-to-all-start.3) | async-done | bytes 131104 | tf_op jit(solution)/shard_map/all_to_all | solution.py:307
  100.5 0.7 sum_z.1
Async XLA Ops:
  2.5 35.0 %all-to-all-start = ((bf16[64,16,128]{2,1,0:T(8,128)(2,1)}), bf16[64,16,128]{2,1,0:T(8,128)(2,1)S(1)}, u32[]{:S(2)}, u32[]{:S(2)}) async-start(bf16[64,16,128]{2,1,0:T(8,128)(2,1)} %pack.1), calls=%async_computation | async-start | bytes 524288 | tf_op jit(solution)/shard_map/all_to_all | solution.py:287
  39.7 6.5 %collective-permute-start = (bf16[2048,128]{1,0:T(8,128)(2,1)S(1)}, bf16[2048,128]{1,0:T(8,128)(2,1)S(1)}, u32[]{:S(2)}, u32[]{:S(2)}) collective-permute-start(bf16[2048,128]{1,0:T(8,128)(2,1)S(1)} %get-tuple-element.15.own), channel_id=1, source_target_pairs={{0,64},{64,0},{1,65},{65,1},{2,66},{66,2},{3,67},{67,3},{4,68},{68... | collective-permute-start | bytes 1572872 | tf_op jit(solution)/shard_map/ppermute | solution.py:295
  86.1 14.4 %all-to-all-start.3 = ((bf16[8,16,512]{2,1,0:T(8,128)(2,1)}), bf16[8,16,512]{2,1,0:T(8,128)(2,1)S(1)}, u32[]{:S(2)}, u32[]{:S(2)}) async-start(bf16[8,16,512]{2,1,0:T(8,128)(2,1)} %sum_far.1), calls=%async_computation.3 | async-start | bytes 262144 | tf_op jit(solution)/shard_map/all_to_all | solution.py:307

commit v5 on v4

--- a/solution.py
+++ b/solution.py
@@ -111,7 +111,7 @@
             ref[0, m % 2, :, lanes] = flat[m * 64 : (m + 1) * 64, :].astype(BF16)
 
 
-def main_body(recv, w_qkv, w_out, bias, send, keep, grads, scr):
+def main_body(recv, w_qkv_tall, w_out, bias, send, keep, grads, scr):
     width = w_out.shape[0]
     scale = 1.0 / math.sqrt(width // HEADS)
     scr[...] = recv[...].reshape(1024, LANES).astype(F32)
@@ -119,9 +119,9 @@
     cot = get_chunks(scr, 1)
     shift_b = shift.astype(BF16)
     cot_b = cot.astype(BF16)
-    wq = w_qkv[...]
+    wq = w_qkv_tall[...]
     wo = w_out[...]
-    projected = nt(shift_b, wq).astype(BF16)
+    projected = nn(shift_b, wq).astype(BF16)
     grad_att = nn(cot_b, wo).astype(BF16)
     first = lax.broadcasted_iota(jnp.int32, (128, LANES), 1) < LANES // 2
     zero = jnp.zeros((128, LANES), BF16)
@@ -175,7 +175,7 @@
         grads[:, p * LANES : (p + 1) * LANES] = part
 
 
-def rows_body(recv, own, grads, w_qkv, w_out, rows_out, scr):
+def rows_body(recv, own, grads, w_qkv_tall, w_out, rows_out, scr):
     width = w_out.shape[0]
     scr[...] = recv[...].reshape(1024, LANES).astype(F32)
     shift = get_chunks(scr, 0)
@@ -184,7 +184,7 @@
         [own[1536 + k * 128 : 1536 + (k + 1) * 128, :] for k in range(width // LANES)], axis=1
     )
     out = shift + nt(attended, w_out[...])
-    grad_in = cot + nn(grads[...], w_qkv[...])
+    grad_in = cot + nt(grads[...], w_qkv_tall[...])
     for k in range(width // LANES):
         lanes = slice(k * LANES, (k + 1) * LANES)
         here = scr.at[k * 256 : (k + 1) * 256]
@@ -253,7 +253,7 @@
         out[core * 16 : (core + 1) * 16, :] = total * gscale
 
 
-def prep_body(pattern, train, w_qkv, w_out, bias, w_qkv_here, w_out_here):
+def prep_body(pattern, train, w_qkv, w_out, bias, w_qkv_tall, w_out_here):
     key = lax.broadcasted_iota(jnp.int32, (128, 128), 0)
     query = lax.broadcasted_iota(jnp.int32, (128, 128), 1)
     key_block = lax.rem(key, 64) // 16
@@ -263,9 +263,13 @@
         for b in range(4):
             here = (query_block == a) & (key_block == b)
             open_block = jnp.where(here, pattern[a, b], open_block)
-    allowed = ((open_block == 1) & (train[...] == 1)) | (key == query)
+    source = 2 * lax.rem(key, 64) + key // 64
+    is_train = jnp.where(query == source, train[...].astype(F32), 0.0)
+    is_train = jnp.sum(is_train, axis=1, keepdims=True) == 1.0
+    allowed = ((open_block == 1) & is_train) | (key == query)
     bias[...] = jnp.where(allowed, 0.0, -jnp.inf).astype(F32)
-    w_qkv_here[...] = w_qkv[...]
+    for e in range(w_qkv.shape[0] // LANES):
+        w_qkv_tall[:, e * LANES : (e + 1) * LANES] = w_qkv[e * LANES : (e + 1) * LANES, :].T
     w_out_here[...] = w_out[...]
 
 
@@ -275,15 +279,18 @@
     (packed,) = call(pack_body, [held(64, 16, LANES)], 4, [scr], (0,), (1, 2, 3), "pack")(
         treated, row_embed, cotangent, treat_vec.reshape(1, -1)
     )
-    train = jnp.transpose(is_train.reshape(64, 2)).reshape(128, 1)
-    bias, w_qkv, w_out = call(
+    bias, w_qkv_tall, w_out = call(
         prep_body,
-        [held(128, 128, dtype=F32), held(*w_qkv.shape), held(*w_out.shape)],
+        [
+            held(128, 128, dtype=F32),
+            held(*w_qkv.shape[::-1]),
+            held(*w_out.shape),
+        ],
         4,
         smem=(0,),
         free=(1, 2, 3),
         name="prep",
-    )(block_pattern, train, w_qkv, w_out)
+    )(block_pattern, is_train, w_qkv, w_out)
     recv = lax.all_to_all(packed, CELL, 0, 0, tiled=True)
     send, keep, grads = call(
         main_body,
@@ -291,10 +298,10 @@
         4,
         [scr],
         name="attend",
-    )(recv, w_qkv, w_out, bias)
+    )(recv, w_qkv_tall, w_out, bias)
     other = lax.ppermute(send, "core", [(0, 1), (1, 0)])
     (rows_out,) = call(rows_body, [held(8, 32, 512)], 5, [scr], name="rows")(
-        recv, send, grads, w_qkv, w_out
+        recv, send, grads, w_qkv_tall, w_out
     )
     (merged,) = call(weight_body, [held(8, 160, 512)], 4, name="weight")(
         keep, send, other, rows_out

time: 102 us -> 101 us (level)
  waiting for transfers between devices: 16.5 us -> 18.7 us
  local copies, waits for them, and re-layouts: 1.5 us -> 0 us
  other arithmetic: 1.32 us -> 0 us
    all_to_all x1, waiting for transfers between devices: 10.9 us -> 13.4 us  [per_device(): recv = lax.all_to_all(packed, CELL, 0, 0, tiled=True)]
    unnamed x1 -> x0, other arithmetic: 1.32 us -> none
  transfers between devices with their start and end apart: 3 -> 3, of which waited for: 3 -> 3; matrix products, arithmetic and copies ran while one was open for 3% -> 0% of each run, Pallas kernels for 3% -> 4%
where the time goes in v5:
time: 101 us
  blocking collectives  38.2 us (38%)
  starting transfers between devices  33.1 us (33%)
  waiting for transfers between devices  18.7 us (19%)
  Pallas kernels  10.1 us (10%)
    all_to_all x1, blocking collectives, per_device(): by_near = lax.all_to_all(merged, NEAR, 0, 0, tiled=True)  20.7 us
    all_to_all x1, starting transfers between devices, per_device(): recv = lax.all_to_all(packed, CELL, 0, 0, tiled=True)  19.6 us
    all_to_all x1, blocking collectives, per_device(): by_far = lax.all_to_all(part_near, FAR, 0, 0, tiled=True)  17.5 us
    all_to_all x1, waiting for transfers between devices, per_device(): recv = lax.all_to_all(packed, CELL, 0, 0, tiled=True)  13.4 us
    pallas_call x9, Pallas kernels, apply(): run(*[a if i in smem or i in free else pltpu.with_memory_space_constraint...  10.1 us
    all_to_all x1, starting transfers between devices, per_device(): by_z = lax.all_to_all(part_far, GRP, 0, 0, tiled=True)  8.62 us
    ppermute x1, starting transfers between devices, per_device(): other = lax.ppermute(send, 'core', [(0, 1), (1, 0)])  4.92 us
    all_to_all x1, waiting for transfers between devices, per_device(): by_z = lax.all_to_all(part_far, GRP, 0, 0, tiled=True)  4.73 us
  transfers between devices with their start and end apart: 3, of which 3 were waited for; matrix products, arithmetic and copies ran while one was open for 0% of the time, Pallas kernels for 4%

profile of v5, /device:TPU:1, one launch (start us, length us, event | category | flops | bytes accessed | tf_op | source)
XLA Modules:
  0.0 100.9 jit_solution(13400766016370767220)
XLA Ops:
  0.6 1.9 %pack.1 = bf16[64,16,128]{2,1,0:T(8,128)(2,1)} custom-call(s32[1,128]{1,0:T(1,128)} %treat_rows.1, bf16[1,2,64,512]{3,2,1,0:T(8,128)(2,1)} %embed.1, bf16[1,2,64,512]{3,2,1,0:T(8,128)(2,1)} %cot.1, f32[1,512]{1,0:T(1,128)} %bitcast.1), custom_call_target="tpu_custom_call" | custom-call | tf_op jit(solution)/shard_map/pack/pallas_call | solution.py:37
  2.5 19.6 %all-to-all-start = ((bf16[64,16,128]{2,1,0:T(8,128)(2,1)}), bf16[64,16,128]{2,1,0:T(8,128)(2,1)S(1)}, u32[]{:S(2)}, u32[]{:S(2)}) async-start(bf16[64,16,128]{2,1,0:T(8,128)(2,1)} %pack.1), calls=%async_computation | async-start | bytes 524288 | tf_op jit(solution)/shard_map/all_to_all | solution.py:294
  22.1 2.0 %prep.1 = (f32[128,128]{1,0:T(8,128)S(1)}, bf16[512,1536]{1,0:T(8,128)(2,1)S(1)}, bf16[512,512]{1,0:T(8,128)(2,1)S(1)}) custom-call(s32[4,4]{1,0:T(4,128)} %pattern.1, s32[1,128]{1,0:T(1,128)} %train.1, bf16[1536,512]{1,0:T(8,128)(2,1)} %w_qkv.1, bf16[512,512]{1,0:T(8,128)(2,1)} %w_out.1), custom_call_target="tpu_custom_call" | custom-call | tf_op jit(solution)/shard_map/prep/pallas_call | solution.py:37
  24.1 13.4 %all-to-all-done.recv = bf16[64,16,128]{2,1,0:T(8,128)(2,1)S(1)} async-done(((bf16[64,16,128]{2,1,0:T(8,128)(2,1)}), bf16[64,16,128]{2,1,0:T(8,128)(2,1)S(1)}, u32[]{:S(2)}, u32[]{:S(2)}) %all-to-all-start) | async-done | bytes 262176 | tf_op jit(solution)/shard_map/all_to_all | solution.py:294
  37.5 2.0 %attend.1 = (bf16[2048,128]{1,0:T(8,128)(2,1)S(1)}, bf16[1024,128]{1,0:T(8,128)(2,1)S(1)}, bf16[128,1536]{1,0:T(8,128)(2,1)S(1)}) custom-call(bf16[64,16,128]{2,1,0:T(8,128)(2,1)S(1)} %all-to-all-done.recv, bf16[512,1536]{1,0:T(8,128)(2,1)S(1)} %get-tuple-element.11.w_qkv_tall, bf16[512,512]{1,0:T(8,128)(2,1)S(1)} %get-tuple-element.12.w_out, ...), custom_call_target="tpu_custom_call" | custom-call | tf_op jit(solution)/shard_map/attend/pallas_call | solution.py:37
  39.5 4.9 %collective-permute-start = (bf16[2048,128]{1,0:T(8,128)(2,1)S(1)}, bf16[2048,128]{1,0:T(8,128)(2,1)S(1)}, u32[]{:S(2)}, u32[]{:S(2)}) collective-permute-start(bf16[2048,128]{1,0:T(8,128)(2,1)S(1)} %get-tuple-element.15.own), channel_id=1, source_target_pairs={{0,64},{64,0},{1,65},{65,1},{2,66},{66,2},{3,67},{67,3},{4,68},{68... | collective-permute-start | bytes 1572872 | tf_op jit(solution)/shard_map/ppermute | solution.py:302
  44.4 0.9 rows.1.rows_out
  45.3 0.6 collective-permute-done.other
  45.9 0.4 weight.1
  46.4 20.7 %all_to_all.20.parts = bf16[8,160,512]{2,1,0:T(8,128)(2,1)S(1)} all-to-all(bf16[8,160,512]{2,1,0:T(8,128)(2,1)S(1)} %weight.1), channel_id=1, replica_groups=mesh['z_lo'=4,'core'=2,'x'=4,'z_hi'=2,'y_hi'=4,'y_lo'=2] {'x','y_lo'}, dimensions={0} | all-to-all | bytes 2621440 | tf_op jit(solution)/shard_map/all_to_all | solution.py:309
  67.1 0.5 sum_near.1
  67.6 17.5 %all_to_all.21.recv.parts = bf16[8,48,512]{2,1,0:T(8,128)(2,1)S(1)} all-to-all(bf16[8,48,512]{2,1,0:T(8,128)(2,1)S(1)} %sum_near.1), channel_id=1, replica_groups=mesh['z_lo'=4,'core'=2,'x'=4,'z_hi'=2,'y_hi'=4,'y_lo'=2] {'z_hi','y_hi'}, dimensions={0} | all-to-all | bytes 786432 | tf_op jit(solution)/shard_map/all_to_all | solution.py:312
  85.1 0.7 sum_far.1
  85.8 8.6 %all-to-all-start.3 = ((bf16[8,16,512]{2,1,0:T(8,128)(2,1)}), bf16[8,16,512]{2,1,0:T(8,128)(2,1)S(1)}, u32[]{:S(2)}, u32[]{:S(2)}) async-start(bf16[8,16,512]{2,1,0:T(8,128)(2,1)} %sum_far.1), calls=%async_computation.3 | async-start | bytes 262144 | tf_op jit(solution)/shard_map/all_to_all | solution.py:314
  94.4 1.1 %unpack.1 = (bf16[1,2,64,512]{3,2,1,0:T(8,128)(2,1)}, bf16[1,2,64,512]{3,2,1,0:T(8,128)(2,1)}) custom-call(bf16[8,48,512]{2,1,0:T(8,128)(2,1)S(1)} %all_to_all.21.recv.parts), custom_call_target="tpu_custom_call" | custom-call | tf_op jit(solution)/shard_map/unpack/pallas_call | solution.py:37
  95.5 4.7 %all-to-all-done.3.parts = bf16[8,16,512]{2,1,0:T(8,128)(2,1)S(1)} async-done(((bf16[8,16,512]{2,1,0:T(8,128)(2,1)}), bf16[8,16,512]{2,1,0:T(8,128)(2,1)S(1)}, u32[]{:S(2)}, u32[]{:S(2)}) %all-to-all-start.3) | async-done | bytes 131104 | tf_op jit(solution)/shard_map/all_to_all | solution.py:314
  100.2 0.7 sum_z.1
Async XLA Ops:
  2.5 35.0 %all-to-all-start = ((bf16[64,16,128]{2,1,0:T(8,128)(2,1)}), bf16[64,16,128]{2,1,0:T(8,128)(2,1)S(1)}, u32[]{:S(2)}, u32[]{:S(2)}) async-start(bf16[64,16,128]{2,1,0:T(8,128)(2,1)} %pack.1), calls=%async_computation | async-start | bytes 524288 | tf_op jit(solution)/shard_map/all_to_all | solution.py:294
  39.5 6.4 %collective-permute-start = (bf16[2048,128]{1,0:T(8,128)(2,1)S(1)}, bf16[2048,128]{1,0:T(8,128)(2,1)S(1)}, u32[]{:S(2)}, u32[]{:S(2)}) collective-permute-start(bf16[2048,128]{1,0:T(8,128)(2,1)S(1)} %get-tuple-element.15.own), channel_id=1, source_target_pairs={{0,64},{64,0},{1,65},{65,1},{2,66},{66,2},{3,67},{67,3},{4,68},{68... | collective-permute-start | bytes 1572872 | tf_op jit(solution)/shard_map/ppermute | solution.py:302
  85.8 14.4 %all-to-all-start.3 = ((bf16[8,16,512]{2,1,0:T(8,128)(2,1)}), bf16[8,16,512]{2,1,0:T(8,128)(2,1)S(1)}, u32[]{:S(2)}, u32[]{:S(2)}) async-start(bf16[8,16,512]{2,1,0:T(8,128)(2,1)} %sum_far.1), calls=%async_computation.3 | async-start | bytes 262144 | tf_op jit(solution)/shard_map/all_to_all | solution.py:314

commit v6 on v5

--- a/solution.py
+++ b/solution.py
@@ -80,18 +80,9 @@
     )
 
 
-def pack_body(treat_rows, embed, cot, treat_vec, send, scr):
-    first = lax.axis_index(CELL) * 2
-    vec = treat_vec[...]
-    shifted = jnp.concatenate(
-        [
-            embed[0, r].astype(F32) + treat_rows[0, first + r].astype(F32) * vec
-            for r in range(2)
-        ],
-        axis=0,
-    )
-    put_chunks(scr, shifted, 0)
-    put_chunks(scr, jnp.concatenate([cot[0, 0], cot[0, 1]], axis=0).astype(F32), 1)
+def pack_body(embed, cot, send, scr):
+    for n, ref in enumerate((embed, cot)):
+        put_chunks(scr, jnp.concatenate([ref[0, 0], ref[0, 1]], axis=0).astype(F32), n)
     send[...] = scr[...].astype(BF16).reshape(64, 16, LANES)
 
 
@@ -111,11 +102,11 @@
             ref[0, m % 2, :, lanes] = flat[m * 64 : (m + 1) * 64, :].astype(BF16)
 
 
-def main_body(recv, w_qkv_tall, w_out, bias, send, keep, grads, scr):
+def main_body(recv, w_qkv_tall, w_out, bias, treatment, send, keep, grads, scr):
     width = w_out.shape[0]
     scale = 1.0 / math.sqrt(width // HEADS)
     scr[...] = recv[...].reshape(1024, LANES).astype(F32)
-    shift = get_chunks(scr, 0)
+    shift = get_chunks(scr, 0) + treatment[...]
     cot = get_chunks(scr, 1)
     shift_b = shift.astype(BF16)
     cot_b = cot.astype(BF16)
@@ -178,7 +169,9 @@
 def rows_body(recv, own, grads, w_qkv_tall, w_out, rows_out, scr):
     width = w_out.shape[0]
     scr[...] = recv[...].reshape(1024, LANES).astype(F32)
-    shift = get_chunks(scr, 0)
+    shift = jnp.concatenate(
+        [own[1024 + k * 128 : 1024 + (k + 1) * 128, :] for k in range(width // LANES)], axis=1
+    ).astype(F32)
     cot = get_chunks(scr, 1)
     attended = jnp.concatenate(
         [own[1536 + k * 128 : 1536 + (k + 1) * 128, :] for k in range(width // LANES)], axis=1
@@ -253,7 +246,7 @@
         out[core * 16 : (core + 1) * 16, :] = total * gscale
 
 
-def prep_body(pattern, train, w_qkv, w_out, bias, w_qkv_tall, w_out_here):
+def prep_body(pattern, train, treated, treat_vec, w_qkv, w_out, bias, treatment, w_qkv_tall, w_out_here):
     key = lax.broadcasted_iota(jnp.int32, (128, 128), 0)
     query = lax.broadcasted_iota(jnp.int32, (128, 128), 1)
     key_block = lax.rem(key, 64) // 16
@@ -264,8 +257,13 @@
             here = (query_block == a) & (key_block == b)
             open_block = jnp.where(here, pattern[a, b], open_block)
     source = 2 * lax.rem(key, 64) + key // 64
-    is_train = jnp.where(query == source, train[...].astype(F32), 0.0)
-    is_train = jnp.sum(is_train, axis=1, keepdims=True) == 1.0
+
+    def column(row):
+        picked = jnp.where(query == source, row[...].astype(F32), 0.0)
+        return jnp.sum(picked, axis=1, keepdims=True)
+
+    is_train = column(train) == 1.0
+    treatment[...] = column(treated) * treat_vec[...]
     allowed = ((open_block == 1) & is_train) | (key == query)
     bias[...] = jnp.where(allowed, 0.0, -jnp.inf).astype(F32)
     for e in range(w_qkv.shape[0] // LANES):
@@ -276,29 +274,30 @@
 def per_device(row_embed, cotangent, w_qkv, w_out, treat_vec, is_train, treated, block_pattern):
     scr = pltpu.VMEM((1024, LANES), F32)
     rows = row_embed.shape
-    (packed,) = call(pack_body, [held(64, 16, LANES)], 4, [scr], (0,), (1, 2, 3), "pack")(
-        treated, row_embed, cotangent, treat_vec.reshape(1, -1)
-    )
-    bias, w_qkv_tall, w_out = call(
+    (packed,) = call(pack_body, [held(64, 16, LANES)], 2, [scr], free=(0, 1), name="pack")(
+        row_embed, cotangent
+    )
+    bias, treatment, w_qkv_tall, w_out = call(
         prep_body,
         [
             held(128, 128, dtype=F32),
+            held(128, w_qkv.shape[1], dtype=F32),
             held(*w_qkv.shape[::-1]),
             held(*w_out.shape),
         ],
-        4,
+        6,
         smem=(0,),
-        free=(1, 2, 3),
+        free=(1, 2, 3, 4, 5),
         name="prep",
-    )(block_pattern, is_train, w_qkv, w_out)
+    )(block_pattern, is_train, treated, treat_vec.reshape(1, -1), w_qkv, w_out)
     recv = lax.all_to_all(packed, CELL, 0, 0, tiled=True)
     send, keep, grads = call(
         main_body,
         [held(2048, LANES), held(1024, LANES), held(128, 1536)],
-        4,
+        5,
         [scr],
         name="attend",
-    )(recv, w_qkv_tall, w_out, bias)
+    )(recv, w_qkv_tall, w_out, bias, treatment)
     other = lax.ppermute(send, "core", [(0, 1), (1, 0)])
     (rows_out,) = call(rows_body, [held(8, 32, 512)], 5, [scr], name="rows")(
         recv, send, grads, w_qkv_tall, w_out

time: 101 us -> 101 us (level)
  no operation moved by 1% of the time
where the time goes in v6:
time: 101 us
  blocking collectives  38.2 us (38%)
  starting transfers between devices  33.1 us (33%)
  waiting for transfers between devices  18.7 us (19%)
  Pallas kernels  10.1 us (10%)
    all_to_all x1, blocking collectives, per_device(): by_near = lax.all_to_all(merged, NEAR, 0, 0, tiled=True)  20.7 us
    all_to_all x1, starting transfers between devices, per_device(): recv = lax.all_to_all(packed, CELL, 0, 0, tiled=True)  19.6 us
    all_to_all x1, blocking collectives, per_device(): by_far = lax.all_to_all(part_near, FAR, 0, 0, tiled=True)  17.6 us
    all_to_all x1, waiting for transfers between devices, per_device(): recv = lax.all_to_all(packed, CELL, 0, 0, tiled=True)  13.4 us
    pallas_call x9, Pallas kernels, apply(): run(*[a if i in smem or i in free else pltpu.with_memory_space_constraint...  10.1 us
    all_to_all x1, starting transfers between devices, per_device(): by_z = lax.all_to_all(part_far, GRP, 0, 0, tiled=True)  8.59 us
    ppermute x1, starting transfers between devices, per_device(): other = lax.ppermute(send, 'core', [(0, 1), (1, 0)])  4.93 us
    all_to_all x1, waiting for transfers between devices, per_device(): by_z = lax.all_to_all(part_far, GRP, 0, 0, tiled=True)  4.73 us
  transfers between devices with their start and end apart: 3, of which 3 were waited for; matrix products, arithmetic and copies ran while one was open for 0% of the time, Pallas kernels for 4%

profile of v6, /device:TPU:1, one launch (start us, length us, event | category | flops | bytes accessed | tf_op | source)
XLA Modules:
  0.0 100.9 jit_solution(5803306397173077694)
XLA Ops:
  0.6 1.8 %pack.1 = bf16[64,16,128]{2,1,0:T(8,128)(2,1)} custom-call(bf16[1,2,64,512]{3,2,1,0:T(8,128)(2,1)} %embed.1, bf16[1,2,64,512]{3,2,1,0:T(8,128)(2,1)} %cot.1), custom_call_target="tpu_custom_call" | custom-call | tf_op jit(solution)/shard_map/pack/pallas_call | solution.py:37
  2.5 19.6 %all-to-all-start = ((bf16[64,16,128]{2,1,0:T(8,128)(2,1)}), bf16[64,16,128]{2,1,0:T(8,128)(2,1)S(1)}, u32[]{:S(2)}, u32[]{:S(2)}) async-start(bf16[64,16,128]{2,1,0:T(8,128)(2,1)} %pack.1), calls=%async_computation | async-start | bytes 524288 | tf_op jit(solution)/shard_map/all_to_all | solution.py:293
  22.0 2.1 %prep.1 = (f32[128,128]{1,0:T(8,128)S(1)}, f32[128,512]{1,0:T(8,128)S(1)}, bf16[512,1536]{1,0:T(8,128)(2,1)S(1)}, bf16[512,512]{1,0:T(8,128)(2,1)S(1)}) custom-call(s32[4,4]{1,0:T(4,128)} %pattern.1, s32[1,128]{1,0:T(1,128)} %train.1, s32[1,128]{1,0:T(1,128)} %treated.1, f32[1,512]{1,0:T(1,128)} %bitcast.1, bf16[1536,512]{1,0:T(8,128)(2,1)} %w_qkv.1, ...), custom_call_target="tpu_custom_call" | custom-call | tf_op jit(solution)/shard_map/prep/pallas_call | solution.py:37
  24.1 13.4 %all-to-all-done.recv = bf16[64,16,128]{2,1,0:T(8,128)(2,1)S(1)} async-done(((bf16[64,16,128]{2,1,0:T(8,128)(2,1)}), bf16[64,16,128]{2,1,0:T(8,128)(2,1)S(1)}, u32[]{:S(2)}, u32[]{:S(2)}) %all-to-all-start) | async-done | bytes 262176 | tf_op jit(solution)/shard_map/all_to_all | solution.py:293
  37.5 2.0 %attend.1 = (bf16[2048,128]{1,0:T(8,128)(2,1)S(1)}, bf16[1024,128]{1,0:T(8,128)(2,1)S(1)}, bf16[128,1536]{1,0:T(8,128)(2,1)S(1)}) custom-call(bf16[64,16,128]{2,1,0:T(8,128)(2,1)S(1)} %all-to-all-done.recv, bf16[512,1536]{1,0:T(8,128)(2,1)S(1)} %get-tuple-element.12.w_qkv_tall, bf16[512,512]{1,0:T(8,128)(2,1)S(1)} %get-tuple-element.13.w_out, ...), custom_call_target="tpu_custom_call" | custom-call | tf_op jit(solution)/shard_map/attend/pallas_call | solution.py:37
  39.5 4.9 %collective-permute-start = (bf16[2048,128]{1,0:T(8,128)(2,1)S(1)}, bf16[2048,128]{1,0:T(8,128)(2,1)S(1)}, u32[]{:S(2)}, u32[]{:S(2)}) collective-permute-start(bf16[2048,128]{1,0:T(8,128)(2,1)S(1)} %get-tuple-element.17.own), channel_id=1, source_target_pairs={{0,64},{64,0},{1,65},{65,1},{2,66},{66,2},{3,67},{67,3},{4,68},{68... | collective-permute-start | bytes 1572872 | tf_op jit(solution)/shard_map/ppermute | solution.py:301
  44.4 0.9 rows.1.rows_out
  45.3 0.6 collective-permute-done.other
  45.9 0.4 weight.1
  46.4 20.7 %all_to_all.20.parts = bf16[8,160,512]{2,1,0:T(8,128)(2,1)S(1)} all-to-all(bf16[8,160,512]{2,1,0:T(8,128)(2,1)S(1)} %weight.1), channel_id=1, replica_groups=mesh['z_lo'=4,'core'=2,'x'=4,'z_hi'=2,'y_hi'=4,'y_lo'=2] {'x','y_lo'}, dimensions={0} | all-to-all | bytes 2621440 | tf_op jit(solution)/shard_map/all_to_all | solution.py:308
  67.1 0.5 sum_near.1
  67.6 17.6 %all_to_all.21.recv.parts = bf16[8,48,512]{2,1,0:T(8,128)(2,1)S(1)} all-to-all(bf16[8,48,512]{2,1,0:T(8,128)(2,1)S(1)} %sum_near.1), channel_id=1, replica_groups=mesh['z_lo'=4,'core'=2,'x'=4,'z_hi'=2,'y_hi'=4,'y_lo'=2] {'z_hi','y_hi'}, dimensions={0} | all-to-all | bytes 786432 | tf_op jit(solution)/shard_map/all_to_all | solution.py:311
  85.2 0.7 sum_far.1
  85.8 8.6 %all-to-all-start.3 = ((bf16[8,16,512]{2,1,0:T(8,128)(2,1)}), bf16[8,16,512]{2,1,0:T(8,128)(2,1)S(1)}, u32[]{:S(2)}, u32[]{:S(2)}) async-start(bf16[8,16,512]{2,1,0:T(8,128)(2,1)} %sum_far.1), calls=%async_computation.3 | async-start | bytes 262144 | tf_op jit(solution)/shard_map/all_to_all | solution.py:313
  94.4 1.1 %unpack.1 = (bf16[1,2,64,512]{3,2,1,0:T(8,128)(2,1)}, bf16[1,2,64,512]{3,2,1,0:T(8,128)(2,1)}) custom-call(bf16[8,48,512]{2,1,0:T(8,128)(2,1)S(1)} %all_to_all.21.recv.parts), custom_call_target="tpu_custom_call" | custom-call | tf_op jit(solution)/shard_map/unpack/pallas_call | solution.py:37
  95.5 4.7 %all-to-all-done.3.parts = bf16[8,16,512]{2,1,0:T(8,128)(2,1)S(1)} async-done(((bf16[8,16,512]{2,1,0:T(8,128)(2,1)}), bf16[8,16,512]{2,1,0:T(8,128)(2,1)S(1)}, u32[]{:S(2)}, u32[]{:S(2)}) %all-to-all-start.3) | async-done | bytes 131104 | tf_op jit(solution)/shard_map/all_to_all | solution.py:313
  100.2 0.7 sum_z.1
Async XLA Ops:
  2.5 35.0 %all-to-all-start = ((bf16[64,16,128]{2,1,0:T(8,128)(2,1)}), bf16[64,16,128]{2,1,0:T(8,128)(2,1)S(1)}, u32[]{:S(2)}, u32[]{:S(2)}) async-start(bf16[64,16,128]{2,1,0:T(8,128)(2,1)} %pack.1), calls=%async_computation | async-start | bytes 524288 | tf_op jit(solution)/shard_map/all_to_all | solution.py:293
  39.5 6.5 %collective-permute-start = (bf16[2048,128]{1,0:T(8,128)(2,1)S(1)}, bf16[2048,128]{1,0:T(8,128)(2,1)S(1)}, u32[]{:S(2)}, u32[]{:S(2)}) collective-permute-start(bf16[2048,128]{1,0:T(8,128)(2,1)S(1)} %get-tuple-element.17.own), channel_id=1, source_target_pairs={{0,64},{64,0},{1,65},{65,1},{2,66},{66,2},{3,67},{67,3},{4,68},{68... | collective-permute-start | bytes 1572872 | tf_op jit(solution)/shard_map/ppermute | solution.py:301
  85.8 14.4 %all-to-all-start.3 = ((bf16[8,16,512]{2,1,0:T(8,128)(2,1)}), bf16[8,16,512]{2,1,0:T(8,128)(2,1)S(1)}, u32[]{:S(2)}, u32[]{:S(2)}) async-start(bf16[8,16,512]{2,1,0:T(8,128)(2,1)} %sum_far.1), calls=%async_computation.3 | async-start | bytes 262144 | tf_op jit(solution)/shard_map/all_to_all | solution.py:313

commit v7 on v6

--- a/solution.py
+++ b/solution.py
@@ -60,19 +60,11 @@
     return jnp.dot(a, b, preferred_element_type=F32)
 
 
-def put_chunks(scr, value, tensor):
-    for r in range(2):
-        for k in range(4):
-            scr[pl.ds(tensor * 8 + r * 4 + k, 64, stride=16), :] = value[
-                r * 64 : (r + 1) * 64, k * LANES : (k + 1) * LANES
-            ]
-
-
 def get_chunks(scr, tensor):
     return jnp.concatenate(
         [
             jnp.concatenate(
-                [scr[pl.ds(tensor * 8 + r * 4 + k, 64, stride=16), :] for k in range(4)], axis=1
+                [scr[pl.ds(r * 8 + tensor * 4 + k, 64, stride=16), :] for k in range(4)], axis=1
             )
             for r in range(2)
         ],
@@ -82,8 +74,10 @@
 
 def pack_body(embed, cot, send, scr):
     for n, ref in enumerate((embed, cot)):
-        put_chunks(scr, jnp.concatenate([ref[0, 0], ref[0, 1]], axis=0).astype(F32), n)
-    send[...] = scr[...].astype(BF16).reshape(64, 16, LANES)
+        value = ref[0, 0].astype(F32)
+        for k in range(4):
+            scr[pl.ds(n * 4 + k, 64, stride=8), :] = value[:, k * LANES : (k + 1) * LANES]
+    send[...] = scr[...].astype(BF16).reshape(64, 8, LANES)
 
 
 def unpack_body(recv, out, grad_in, *scr):
@@ -274,9 +268,16 @@
 def per_device(row_embed, cotangent, w_qkv, w_out, treat_vec, is_train, treated, block_pattern):
     scr = pltpu.VMEM((1024, LANES), F32)
     rows = row_embed.shape
-    (packed,) = call(pack_body, [held(64, 16, LANES)], 2, [scr], free=(0, 1), name="pack")(
-        row_embed, cotangent
-    )
+    row = pl.BlockSpec((1, 1) + rows[2:], lambda r: (0, r, 0, 0))
+    packed = pl.pallas_call(
+        pack_body,
+        grid=(2,),
+        out_shape=jax.ShapeDtypeStruct((64, 16, LANES), BF16),
+        in_specs=[row, row],
+        out_specs=pl.BlockSpec((64, 8, LANES), lambda r: (0, r, 0)),
+        scratch_shapes=[pltpu.VMEM((512, LANES), F32)],
+        name="pack",
+    )(row_embed, cotangent)
     bias, treatment, w_qkv_tall, w_out = call(
         prep_body,
         [

time: 101 us -> 101 us (level)
    pallas_call x9 -> x8, Pallas kernels: 10.1 us -> 8.28 us  [apply(): run(*[a if i in smem or i in free else pltpu.with_memory_space_constraint...]
    pallas_call x0 -> x1, Pallas kernels: none -> 1.67 us  [per_device(): pl.pallas_call(pack_body, grid=(2,), out_shape=jax.ShapeDtypeStruct((64,...]
where the time goes in v7:
time: 101 us
  blocking collectives  38.2 us (38%)
  starting transfers between devices  33.1 us (33%)
  waiting for transfers between devices  18.7 us (19%)
  Pallas kernels  9.95 us (10%)
    all_to_all x1, blocking collectives, per_device(): by_near = lax.all_to_all(merged, NEAR, 0, 0, tiled=True)  20.7 us
    all_to_all x1, starting transfers between devices, per_device(): recv = lax.all_to_all(packed, CELL, 0, 0, tiled=True)  19.6 us
    all_to_all x1, blocking collectives, per_device(): by_far = lax.all_to_all(part_near, FAR, 0, 0, tiled=True)  17.5 us
    all_to_all x1, waiting for transfers between devices, per_device(): recv = lax.all_to_all(packed, CELL, 0, 0, tiled=True)  13.4 us
    all_to_all x1, starting transfers between devices, per_device(): by_z = lax.all_to_all(part_far, GRP, 0, 0, tiled=True)  8.61 us
    pallas_call x8, Pallas kernels, apply(): run(*[a if i in smem or i in free else pltpu.with_memory_space_constraint...  8.28 us
    ppermute x1, starting transfers between devices, per_device(): other = lax.ppermute(send, 'core', [(0, 1), (1, 0)])  4.93 us
    all_to_all x1, waiting for transfers between devices, per_device(): by_z = lax.all_to_all(part_far, GRP, 0, 0, tiled=True)  4.73 us
  transfers between devices with their start and end apart: 3, of which 3 were waited for; matrix products, arithmetic and copies ran while one was open for 0% of the time, Pallas kernels for 4%

profile of v7, /device:TPU:1, one launch (start us, length us, event | category | flops | bytes accessed | tf_op | source)
XLA Modules:
  0.0 100.7 jit_solution(3423293021488518801)
XLA Ops:
  0.6 1.7 %pack.1 = bf16[64,16,128]{2,1,0:T(8,128)(2,1)} custom-call(bf16[1,2,64,512]{3,2,1,0:T(8,128)(2,1)} %embed.1, bf16[1,2,64,512]{3,2,1,0:T(8,128)(2,1)} %cot.1), custom_call_target="tpu_custom_call" | custom-call | tf_op jit(solution)/shard_map/pack/pallas_call | solution.py:272
  2.3 19.6 %all-to-all-start = ((bf16[64,16,128]{2,1,0:T(8,128)(2,1)}), bf16[64,16,128]{2,1,0:T(8,128)(2,1)S(1)}, u32[]{:S(2)}, u32[]{:S(2)}) async-start(bf16[64,16,128]{2,1,0:T(8,128)(2,1)} %pack.1), calls=%async_computation | async-start | bytes 524288 | tf_op jit(solution)/shard_map/all_to_all | solution.py:294
  21.9 2.1 %prep.1 = (f32[128,128]{1,0:T(8,128)S(1)}, f32[128,512]{1,0:T(8,128)S(1)}, bf16[512,1536]{1,0:T(8,128)(2,1)S(1)}, bf16[512,512]{1,0:T(8,128)(2,1)S(1)}) custom-call(s32[4,4]{1,0:T(4,128)} %pattern.1, s32[1,128]{1,0:T(1,128)} %train.1, s32[1,128]{1,0:T(1,128)} %treated.1, f32[1,512]{1,0:T(1,128)} %bitcast.1, bf16[1536,512]{1,0:T(8,128)(2,1)} %w_qkv.1, ...), custom_call_target="tpu_custom_call" | custom-call | tf_op jit(solution)/shard_map/prep/pallas_call | solution.py:37
  24.0 13.4 %all-to-all-done.recv = bf16[64,16,128]{2,1,0:T(8,128)(2,1)S(1)} async-done(((bf16[64,16,128]{2,1,0:T(8,128)(2,1)}), bf16[64,16,128]{2,1,0:T(8,128)(2,1)S(1)}, u32[]{:S(2)}, u32[]{:S(2)}) %all-to-all-start) | async-done | bytes 262176 | tf_op jit(solution)/shard_map/all_to_all | solution.py:294
  37.3 2.0 %attend.1 = (bf16[2048,128]{1,0:T(8,128)(2,1)S(1)}, bf16[1024,128]{1,0:T(8,128)(2,1)S(1)}, bf16[128,1536]{1,0:T(8,128)(2,1)S(1)}) custom-call(bf16[64,16,128]{2,1,0:T(8,128)(2,1)S(1)} %all-to-all-done.recv, bf16[512,1536]{1,0:T(8,128)(2,1)S(1)} %get-tuple-element.12.w_qkv_tall, bf16[512,512]{1,0:T(8,128)(2,1)S(1)} %get-tuple-element.13.w_out, ...), custom_call_target="tpu_custom_call" | custom-call | tf_op jit(solution)/shard_map/attend/pallas_call | solution.py:37
  39.3 4.9 %collective-permute-start = (bf16[2048,128]{1,0:T(8,128)(2,1)S(1)}, bf16[2048,128]{1,0:T(8,128)(2,1)S(1)}, u32[]{:S(2)}, u32[]{:S(2)}) collective-permute-start(bf16[2048,128]{1,0:T(8,128)(2,1)S(1)} %get-tuple-element.17.own), channel_id=1, source_target_pairs={{0,64},{64,0},{1,65},{65,1},{2,66},{66,2},{3,67},{67,3},{4,68},{68... | collective-permute-start | bytes 1572872 | tf_op jit(solution)/shard_map/ppermute | solution.py:302
  44.2 0.9 rows.1.rows_out
  45.1 0.7 collective-permute-done.other
  45.7 0.4 weight.1
  46.2 20.7 %all_to_all.20.parts = bf16[8,160,512]{2,1,0:T(8,128)(2,1)S(1)} all-to-all(bf16[8,160,512]{2,1,0:T(8,128)(2,1)S(1)} %weight.1), channel_id=1, replica_groups=mesh['z_lo'=4,'core'=2,'x'=4,'z_hi'=2,'y_hi'=4,'y_lo'=2] {'x','y_lo'}, dimensions={0} | all-to-all | bytes 2621440 | tf_op jit(solution)/shard_map/all_to_all | solution.py:309
  66.9 0.5 sum_near.1
  67.4 17.5 %all_to_all.21.recv.parts = bf16[8,48,512]{2,1,0:T(8,128)(2,1)S(1)} all-to-all(bf16[8,48,512]{2,1,0:T(8,128)(2,1)S(1)} %sum_near.1), channel_id=1, replica_groups=mesh['z_lo'=4,'core'=2,'x'=4,'z_hi'=2,'y_hi'=4,'y_lo'=2] {'z_hi','y_hi'}, dimensions={0} | all-to-all | bytes 786432 | tf_op jit(solution)/shard_map/all_to_all | solution.py:312
  85.0 0.7 sum_far.1
  85.6 8.6 %all-to-all-start.3 = ((bf16[8,16,512]{2,1,0:T(8,128)(2,1)}), bf16[8,16,512]{2,1,0:T(8,128)(2,1)S(1)}, u32[]{:S(2)}, u32[]{:S(2)}) async-start(bf16[8,16,512]{2,1,0:T(8,128)(2,1)} %sum_far.1), calls=%async_computation.3 | async-start | bytes 262144 | tf_op jit(solution)/shard_map/all_to_all | solution.py:314
  94.2 1.1 %unpack.1 = (bf16[1,2,64,512]{3,2,1,0:T(8,128)(2,1)}, bf16[1,2,64,512]{3,2,1,0:T(8,128)(2,1)}) custom-call(bf16[8,48,512]{2,1,0:T(8,128)(2,1)S(1)} %all_to_all.21.recv.parts), custom_call_target="tpu_custom_call" | custom-call | tf_op jit(solution)/shard_map/unpack/pallas_call | solution.py:37
  95.3 4.7 %all-to-all-done.3.parts = bf16[8,16,512]{2,1,0:T(8,128)(2,1)S(1)} async-done(((bf16[8,16,512]{2,1,0:T(8,128)(2,1)}), bf16[8,16,512]{2,1,0:T(8,128)(2,1)S(1)}, u32[]{:S(2)}, u32[]{:S(2)}) %all-to-all-start.3) | async-done | bytes 131104 | tf_op jit(solution)/shard_map/all_to_all | solution.py:314
  100.1 0.7 sum_z.1
Async XLA Ops:
  2.3 35.0 %all-to-all-start = ((bf16[64,16,128]{2,1,0:T(8,128)(2,1)}), bf16[64,16,128]{2,1,0:T(8,128)(2,1)S(1)}, u32[]{:S(2)}, u32[]{:S(2)}) async-start(bf16[64,16,128]{2,1,0:T(8,128)(2,1)} %pack.1), calls=%async_computation | async-start | bytes 524288 | tf_op jit(solution)/shard_map/all_to_all | solution.py:294
  39.3 6.5 %collective-permute-start = (bf16[2048,128]{1,0:T(8,128)(2,1)S(1)}, bf16[2048,128]{1,0:T(8,128)(2,1)S(1)}, u32[]{:S(2)}, u32[]{:S(2)}) collective-permute-start(bf16[2048,128]{1,0:T(8,128)(2,1)S(1)} %get-tuple-element.17.own), channel_id=1, source_target_pairs={{0,64},{64,0},{1,65},{65,1},{2,66},{66,2},{3,67},{67,3},{4,68},{68... | collective-permute-start | bytes 1572872 | tf_op jit(solution)/shard_map/ppermute | solution.py:302
  85.6 14.4 %all-to-all-start.3 = ((bf16[8,16,512]{2,1,0:T(8,128)(2,1)}), bf16[8,16,512]{2,1,0:T(8,128)(2,1)S(1)}, u32[]{:S(2)}, u32[]{:S(2)}) async-start(bf16[8,16,512]{2,1,0:T(8,128)(2,1)} %sum_far.1), calls=%async_computation.3 | async-start | bytes 262144 | tf_op jit(solution)/shard_map/all_to_all | solution.py:314
